TPU v7x, 32 devices: a whole 2x2x4 slice. The times are simulated.
32 devices in a mesh: wshard: 4 (over y, x), seq: 8 (over z, core).
Axes of the slice: x: 2, y: 2, z: 4, core: 2. Of those that a mesh axis runs over, the one named last changes fastest.
Arguments:
- block_input: bfloat16 [8, 1024, 1536], P('wshard', 'seq'), may hold values from -6 to 6
- cotangent: bfloat16 [8, 1024, 1536], P('wshard', 'seq'), may hold values from -6 to 6
- norm_gain: bfloat16 [1536], P('wshard'), may hold values from 0.5 to 1.5
- norm_mean: float32 [1536], P(('wshard', 'seq')), may hold values from -16 to 16
- norm_square: float32 [1536], P(('wshard', 'seq')), may hold values from 0.16384 to 1.6384
- inproj_weight: bfloat16 [1536, 6448], P('wshard'), may hold values from -0.15625 to 0.15625
- inproj_mean: float32 [1536, 6448], P(('wshard', 'seq')), may hold values from -16 to 16
- inproj_square: float32 [1536, 6448], P(('wshard', 'seq')), may hold values from 0.16384 to 1.6384
- conv_params: bfloat16 [5, 3328], P(None, 'wshard'), may hold values from -0.5 to 0.5
- conv_mean: float32 [5, 3328], P(None, ('wshard', 'seq')), may hold values from -16 to 16
- conv_square: float32 [5, 3328], P(None, ('wshard', 'seq')), may hold values from 0.16384 to 1.6384
- head_params: bfloat16 [3, 48], P(None, 'wshard'), may hold values from -7 to 2.8, as said below
- head_mean: float32 [3, 48], P(None, 'wshard'), may hold values from -16 to 16
- head_square: float32 [3, 48], P(None, 'wshard'), may hold values from 0.16384 to 1.6384
- gate_gain: bfloat16 [3072], P('wshard'), may hold values from 0.5 to 1.5
- gate_mean: float32 [3072], P(('wshard', 'seq')), may hold values from -16 to 16
- gate_square: float32 [3072], P(('wshard', 'seq')), may hold values from 0.16384 to 1.6384
- outproj_weight: bfloat16 [3072, 1536], P('wshard'), may hold values from -0.109375 to 0.109375
- outproj_mean: float32 [3072, 1536], P(('wshard', 'seq')), may hold values from -16 to 16
- outproj_square: float32 [3072, 1536], P(('wshard', 'seq')), may hold values from 0.16384 to 1.6384
Outputs:
- block_output: float32 [8, 1024, 1536], P('wshard', 'seq')
- input_grad: float32 [8, 1024, 1536], P('wshard', 'seq')
- norm_grad: float32 [1536], P(('wshard', 'seq'))
- norm_newmean: float32 [1536], P(('wshard', 'seq'))
- norm_newsquare: float32 [1536], P(('wshard', 'seq'))
- norm_update: float32 [1536], P(('wshard', 'seq'))
- inproj_grad: float32 [1536, 6448], P(('wshard', 'seq'))
- inproj_newmean: float32 [1536, 6448], P(('wshard', 'seq'))
- inproj_newsquare: float32 [1536, 6448], P(('wshard', 'seq'))
- inproj_update: float32 [1536, 6448], P(('wshard', 'seq'))
- conv_grad: float32 [5, 3328], P(None, ('wshard', 'seq'))
- conv_newmean: float32 [5, 3328], P(None, ('wshard', 'seq'))
- conv_newsquare: float32 [5, 3328], P(None, ('wshard', 'seq'))
- conv_update: float32 [5, 3328], P(None, ('wshard', 'seq'))
- head_grad: float32 [3, 48], P(None, 'wshard')
- head_newmean: float32 [3, 48], P(None, 'wshard')
- head_newsquare: float32 [3, 48], P(None, 'wshard')
- head_update: float32 [3, 48], P(None, 'wshard')
- gate_grad: float32 [3072], P(('wshard', 'seq'))
- gate_newmean: float32 [3072], P(('wshard', 'seq'))
- gate_newsquare: float32 [3072], P(('wshard', 'seq'))
- gate_update: float32 [3072], P(('wshard', 'seq'))
- outproj_grad: float32 [3072, 1536], P(('wshard', 'seq'))
- outproj_newmean: float32 [3072, 1536], P(('wshard', 'seq'))
- outproj_newsquare: float32 [3072, 1536], P(('wshard', 'seq'))
- outproj_update: float32 [3072, 1536], P(('wshard', 'seq'))
Inputs may be any that keep to these rules, and one draw needn't show every extreme that they name: `head_params`: row 0 holds logarithms of decay rates, row 1 step biases, row 2 skip factors.
All inputs are finite; a program needn't handle non-finite values.
Results may differ from a plain program's by a relative error of at most 0.012.
The roundings to bfloat16 on the way count: a program that leaves them out, or rounds other values in their place, can miss the bound.
Values may be sent and summed in bfloat16 or wider, within the bound.
No kernel may reach another device: no remote copies, remote signals or barrier semaphores. Data moves between devices by JAX's collectives and lax.ppermute only.
A program may use at most 256 MiB of HBM per device.

v0:
```python
import functools

import jax
import jax.numpy as jnp
from jax import lax
from jax.experimental import pallas as pl
from jax.experimental.pallas import tpu as pltpu
from jax.sharding import PartitionSpec as P

norm_eps = 1e-05
adam_eps = 1e-08
learn_rate = 0.02
beta_one = 0.9
beta_two = 0.999
first_fix = 1.0 - 0.9**10
second_fix = 1.0 - 0.999**10

f32 = jnp.float32
bf16 = jnp.bfloat16
Q = 128
HP = 16
FLOOR = -1e30
MIB = 1024 * 1024


def dot_nn(a, b):
    return lax.dot_general(a, b, (((1,), (0,)), ((), ())), preferred_element_type=f32)


def dot_nt(a, b):
    return lax.dot_general(a, b, (((1,), (1,)), ((), ())), preferred_element_type=f32)


def dot_tn(a, b):
    return lax.dot_general(a, b, (((0,), (0,)), ((), ())), preferred_element_type=f32)


def sigmoid(a):
    return 1.0 / (1.0 + jnp.exp(-a))


def lanes(shape):
    return lax.broadcasted_iota(jnp.int32, shape, 1)


def earlier_by(current, previous, lane, shift):
    return pltpu.roll(jnp.where(lane >= Q - shift, previous, current), shift, 1)


def later_by(current, following, lane, shift):
    return pltpu.roll(jnp.where(lane < shift, following, current), Q - shift, 1)


def running_sum(a, lane):
    shift = 1
    while shift < Q:
        a = a + jnp.where(lane >= shift, pltpu.roll(a, shift, 1), 0.0)
        shift *= 2
    return a


def running_sum_back(a, lane):
    shift = 1
    while shift < Q:
        a = a + jnp.where(lane < Q - shift, pltpu.roll(a, Q - shift, 1), 0.0)
        shift *= 2
    return a


def join_weight(own_width, channels, core, own_ref, other_ref, weight_ref):
    shards, _, depth = own_ref.shape
    for even in range(2):

        @pl.when(core == even)
        def _(first=(own_ref, other_ref)[even], second=(other_ref, own_ref)[even]):
            for at in range(shards):
                here = slice(at * depth, (at + 1) * depth)
                low = 2 * own_width
                weight_ref[:own_width, here] = first[at, :own_width, :]
                weight_ref[own_width:low, here] = second[at, :own_width, :]
                weight_ref[low : low + Q, here] = first[at, own_width : own_width + Q, :]
                weight_ref[low + Q : low + 2 * Q, here] = second[at, own_width : own_width + Q, :]
                weight_ref[low + 2 * Q :, here] = own_ref[at, own_width + Q : own_width + Q + HP, :]


def mixer_forward(own_width, heads, kernel_len, places, start, assemble, order_ref, *refs):
    token_refs = refs[:places]
    gain_ref, chan_ref, head_ref = refs[places : places + 3]
    given = refs[places + 3 : -14]
    (
        weight_out,
        normed_ref,
        gates_ref,
        values_ref,
        conv_ref,
        sent_ref,
        table_ref,
        state_ref,
        before,
        state,
        active,
        steps,
        inter,
        scaled,
    ) = refs[-14:]
    channels = chan_ref.shape[0]
    width = own_width // heads
    token_block = normed_ref.shape[0]

    @pl.when(pl.program_id(0) == 0)
    def _():
        before[...] = given[1][...] if start else jnp.zeros_like(before)
        state[...] = given[2][...] if start else jnp.zeros_like(state)
        if not assemble:
            weight_out[...] = jnp.zeros_like(weight_out)
        else:
            join_weight(own_width, channels, order_ref[places], *given[:2], weight_out)

    for piece in range(places):

        @pl.when(order_ref[start + pl.program_id(0)] == piece)
        def _(token_ref=token_refs[piece]):
            tokens = token_ref[...].astype(f32)
            scale = lax.rsqrt(jnp.mean(tokens * tokens, axis=1, keepdims=True) + norm_eps)
            normed_ref[...] = (tokens * scale * gain_ref[...]).astype(bf16)

    weight_ref = weight_out if assemble else given[0]
    normed = normed_ref[...]
    gates_ref[...] = dot_nt(weight_ref[0:own_width, :], normed)
    values_ref[...] = dot_nt(weight_ref[own_width : own_width + channels, :], normed).astype(bf16)
    steps[...] = dot_nt(weight_ref[own_width + channels :, :], normed).astype(bf16).astype(f32)
    lane = lanes((Q, Q))
    lane_head = lanes((HP, Q))
    causal = lax.broadcasted_iota(jnp.int32, (Q, Q), 0) <= lane

    def block(at, carry):
        here = pl.ds(pl.multiple_of(at * Q, Q), Q)

        def convolve(tile, inner):
            rows = pl.ds(pl.multiple_of(tile * Q, Q), Q)
            raw = values_ref[rows, here]
            current = raw.astype(f32)
            previous = before[rows, :].astype(f32)
            taps = chan_ref[rows, :]
            out = taps[:, kernel_len : kernel_len + 1] + taps[:, kernel_len - 1 : kernel_len] * current
            for shift in range(1, kernel_len):
                tap = kernel_len - 1 - shift
                out = out + taps[:, tap : tap + 1] * earlier_by(current, previous, lane, shift)
            before[rows, :] = raw
            conv_ref[rows, here] = out
            active[rows, :] = out * sigmoid(out)
            return inner

        lax.fori_loop(0, channels // Q, convolve, 0, unroll=True)
        drive = steps[:, here] + head_ref[:, 1:2]
        step = jnp.maximum(drive, 0.0) + jnp.log1p(jnp.exp(-jnp.abs(drive)))
        within = running_sum(step * head_ref[:, 0:1], lane_head)
        table_ref[0, :, here] = step
        table_ref[1, :, here] = within
        table_ref[2, :, here] = sigmoid(drive)
        within_col = jnp.transpose(within)
        total = within[:, Q - 1 : Q]
        grow = jnp.exp(within)
        tail = jnp.exp(total - within) * step
        total_decay = jnp.exp(total)
        b_rows = jnp.transpose(active[own_width : own_width + Q, :]).astype(bf16)
        c_cols = active[own_width + Q : own_width + 2 * Q, :].astype(bf16)
        scores = dot_nn(b_rows, c_cols)
        held = state[...].astype(bf16)
        state_ref[at] = held
        inter[...] = dot_nn(held, c_cols)
        for head in range(heads):
            rows = slice(head * width, (head + 1) * width)
            x = active[rows, :]
            decay = jnp.exp(
                jnp.where(causal, within[head : head + 1, :] - within_col[:, head : head + 1], FLOOR)
            )
            weights = (decay * scores).astype(bf16)
            driven = (x * step[head : head + 1, :]).astype(bf16)
            mixed = dot_nn(driven, weights)
            mixed = mixed + inter[rows, :] * grow[head : head + 1, :]
            mixed = mixed + chan_ref[rows, 6:7] * x
            sent_ref[rows, here] = mixed.astype(bf16)
            scaled[rows, :] = (x * tail[head : head + 1, :]).astype(bf16)
            state[rows, :] = state[rows, :] * total_decay[head : head + 1, :]
        state[...] += dot_nn(scaled[...], b_rows)
        return carry

    lax.fori_loop(0, token_block // Q, block, 0, unroll=True)


def gate_statistics(places, order_ref, gates_ref, sent_ref, *refs):
    cot_refs = refs[:places]
    weight_ref, chan_ref, cot_all, dbranch_ref, stat_ref = refs[places:]
    for piece in range(places):

        @pl.when(order_ref[pl.program_id(0)] == piece)
        def _(cot_ref=cot_refs[piece]):
            cot_all[...] = cot_ref[...]

    dbranch = dot_nt(weight_ref[...], cot_all[...])
    dbranch_ref[...] = dbranch
    gates = gates_ref[...]
    gated = sent_ref[...].astype(f32) * (gates * sigmoid(gates))
    square = jnp.sum(gated * gated, axis=0, keepdims=True)
    cross = jnp.sum(gated * (dbranch * chan_ref[0 : gates.shape[0], 7:8]), axis=0, keepdims=True)
    stat_ref[...] = jnp.concatenate([square, cross, jnp.zeros((6, square.shape[1]), f32)], axis=0)


def gate_backward(
    order_ref, gates_ref, sent_ref, dbranch_ref, stat_ref, chan_ref, dsent_ref, dgates_ref, branch_ref
):
    grms = stat_ref[0:1, :]
    pull = stat_ref[1:2, :]

    def gate(tile, carry):
        rows = pl.ds(pl.multiple_of(tile * Q, Q), Q)
        gates = gates_ref[rows, :]
        sent = sent_ref[rows, :].astype(f32)
        gain = chan_ref[rows, 7:8]
        sig = sigmoid(gates)
        swish = gates * sig
        gated = sent * swish
        dgated = grms * (dbranch_ref[rows, :] * gain - gated * pull)
        dsent_ref[rows, :] = (dgated * swish).astype(bf16)
        dgates_ref[rows, :] = (dgated * sent * sig * (1.0 + gates * (1.0 - sig))).astype(bf16)
        branch_ref[rows, :] = (gated * grms * gain).astype(bf16)
        return carry

    lax.fori_loop(0, gates_ref.shape[0] // Q, gate, 0, unroll=True)


def mixer_backward(
    own_width,
    heads,
    kernel_len,
    order_ref,
    dsent_ref,
    conv_ref,
    values_ref,
    table_ref,
    state_ref,
    chan_ref,
    head_ref,
    *refs,
):
    (
        dproj_ref,
        conv_sum,
        head_acc,
        conv_acc,
        adjoint,
        following,
        active,
        dactive,
        inter,
        reach,
        driven,
        tailed,
        rows_scr,
    ) = refs
    channels = chan_ref.shape[0]
    width = own_width // heads
    token_block = dsent_ref.shape[1]

    @pl.when(pl.program_id(0) == 0)
    def _():
        for held in (conv_acc, head_acc, adjoint, following):
            held[...] = jnp.zeros_like(held)
        rows_scr[...] = jnp.zeros_like(rows_scr)

    lane = lanes((Q, Q))
    sub = lax.broadcasted_iota(jnp.int32, (Q, Q), 0)
    lane_head = lanes((HP, Q))
    causal = sub >= lane
    strict = (sub < lane).astype(bf16)

    def block(index, carry):
        at = token_block // Q - 1 - index
        here = pl.ds(pl.multiple_of(at * Q, Q), Q)

        def activate(tile, inner):
            rows = pl.ds(pl.multiple_of(tile * Q, Q), Q)
            conv = conv_ref[rows, here]
            active[rows, :] = conv * sigmoid(conv)
            return inner

        lax.fori_loop(0, channels // Q, activate, 0, unroll=True)
        step = table_ref[0, :, here]
        within = table_ref[1, :, here]
        within_col = jnp.transpose(within)
        total = within[:, Q - 1 : Q]
        grow = jnp.exp(within)
        fade = jnp.exp(total - within)
        tail = fade * step
        total_decay = jnp.exp(total)
        b_cols_f = active[own_width : own_width + Q, :]
        c_cols_f = active[own_width + Q : own_width + 2 * Q, :]
        b_cols = b_cols_f.astype(bf16)
        c_cols = c_cols_f.astype(bf16)
        c_rows = jnp.transpose(c_cols_f).astype(bf16)
        scores = dot_nn(c_rows, b_cols)
        held = state_ref[at]
        after = adjoint[...].astype(bf16)
        inter[...] = dot_nn(held, c_cols)
        reach[...] = dot_nn(after, b_cols)
        dscores = jnp.zeros((Q, Q), f32)
        blank = jnp.zeros((width, Q), bf16)
        for pair in range(heads // 2):
            turned = jnp.transpose(dsent_ref[pair * 2 * width : (pair + 1) * 2 * width, here].astype(f32)).astype(bf16)
            for half in range(2):
                head = 2 * pair + half
                rows = slice(head * width, (head + 1) * width)
                one = slice(head, head + 1)
                x = active[rows, :]
                x_low = x.astype(bf16)
                grad_low = dsent_ref[rows, here]
                grad = grad_low.astype(f32)
                decay = jnp.exp(
                    jnp.where(causal, within_col[:, head : head + 1] - within[one, :], FLOOR)
                )
                lone = jnp.concatenate([x_low, blank] if half == 0 else [blank, x_low], axis=0)
                dweights = dot_nn(turned, lone)
                spread = decay * dweights * step[one, :]
                dscores = dscores + spread
                crossing = dot_nn((spread * scores).astype(bf16), strict)
                rows_scr[0, one, :] = jnp.sum(jnp.where(causal, crossing, 0.0), axis=0, keepdims=True)
                far = reach[rows, :]
                back = dot_nn(grad_low, (decay * scores).astype(bf16)) + far * fade[one, :]
                rows_scr[1, one, :] = jnp.sum(x * back, axis=0, keepdims=True)
                rows_scr[2, one, :] = jnp.sum(x * far, axis=0, keepdims=True) * tail[one, :]
                rows_scr[3, one, :] = jnp.sum(grad * inter[rows, :], axis=0, keepdims=True) * grow[one, :]
                rows_scr[4, one, :] = jnp.sum(grad * x, axis=0, keepdims=True)
                old = adjoint[rows, :]
                rows_scr[5, one, :] = jnp.sum(old * held[rows, :].astype(f32), axis=0, keepdims=True)
                dactive[rows, :] = back * step[one, :] + chan_ref[rows, 6:7] * grad
                driven[rows, :] = (grad * grow[one, :]).astype(bf16)
                tailed[rows, :] = (x * tail[one, :]).astype(bf16)
                adjoint[rows, :] = old * total_decay[one, :]
        dlow = dscores.astype(bf16)
        dactive[own_width : own_width + Q, :] = dot_nn(c_cols, dlow) + dot_tn(after, tailed[...])
        dactive[own_width + Q : own_width + 2 * Q, :] = dot_nt(b_cols, dlow) + dot_tn(held, driven[...])
        adjoint[...] += dot_nn(driven[...], c_rows)
        ahead = rows_scr[2]
        dlog = (
            rows_scr[0]
            + running_sum_back(rows_scr[3], lane_head)
            + (running_sum(ahead, lane_head) - ahead)
            + total_decay * jnp.sum(rows_scr[5], axis=1, keepdims=True)
        )
        dstep = (rows_scr[1] + head_ref[:, 0:1] * dlog) * table_ref[2, :, here]
        dproj_ref[channels:, here] = dstep.astype(bf16)
        head_acc[0] += step * dlog
        head_acc[1] += dstep
        head_acc[2] += rows_scr[4]

        def convolve(tile, inner):
            rows = pl.ds(pl.multiple_of(tile * Q, Q), Q)
            conv = conv_ref[rows, here]
            sig = sigmoid(conv)
            dconv = dactive[rows, :] * sig * (1.0 + conv * (1.0 - sig))
            taps = chan_ref[rows, :]
            raw = values_ref[rows, here].astype(f32)
            nxt = following[rows, :]
            dvalue = taps[:, kernel_len - 1 : kernel_len] * dconv
            conv_acc[kernel_len - 1, rows, :] += raw * dconv
            for shift in range(1, kernel_len):
                tap = kernel_len - 1 - shift
                moved = later_by(dconv, nxt, lane, shift)
                dvalue = dvalue + taps[:, tap : tap + 1] * moved
                conv_acc[tap, rows, :] += raw * moved
            conv_acc[kernel_len, rows, :] += dconv
            following[rows, :] = dconv
            dproj_ref[rows, here] = dvalue.astype(bf16)
            return inner

        lax.fori_loop(0, channels // Q, convolve, 0, unroll=True)
        return carry

    lax.fori_loop(0, token_block // Q, block, 0, unroll=True)

    @pl.when(pl.program_id(0) == pl.num_programs(0) - 1)
    def _():
        ones = jnp.ones((8, Q), f32)
        for tap in range(kernel_len + 1):
            total = lax.dot_general(
                ones,
                conv_acc[tap],
                (((1,), (1,)), ((), ())),
                precision=lax.Precision.HIGHEST,
                preferred_element_type=f32,
            )
            conv_sum[tap : tap + 1, :] = total[0:1, :]


def run_forward(
    order, tokens, gain, chan, head_table, own_width, heads, kernel_len, start, count, weight, carry, written
):
    places = len(tokens)
    token_block, model_width = tokens[0].shape
    channels = chan.shape[0]
    full = places * token_block
    weight_shape = (own_width + channels + HP, model_width)
    assemble = len(weight) == 2
    solid = lambda x: pl.BlockSpec(x.shape, lambda k, order: (0,) * x.ndim)
    fixed = lambda k, order: (0, 0)
    cols = lambda k, order: (0, start + k)
    stored = lambda k, order: (order[start + k], 0, 0)
    spec = pltpu.PrefetchScalarGridSpec(
        num_scalar_prefetch=1,
        grid=(count,),
        in_specs=[solid(x) for x in (*tokens, gain, chan, head_table, *weight, *carry)]
        + [pl.BlockSpec(memory_space=pl.ANY)] * len(written),
        out_specs=[
            pl.BlockSpec(weight_shape if assemble else (8, Q), fixed),
            pl.BlockSpec((None, token_block, model_width), stored),
            pl.BlockSpec((own_width, token_block), cols),
            pl.BlockSpec((channels, token_block), cols),
            pl.BlockSpec((channels, token_block), cols),
            pl.BlockSpec((own_width, token_block), cols),
            pl.BlockSpec((3, HP, token_block), lambda k, order: (0, 0, start + k)),
            pl.BlockSpec((token_block // Q, own_width, Q), lambda k, order: (start + k, 0, 0)),
            pl.BlockSpec((channels, Q), fixed),
            pl.BlockSpec((own_width, Q), fixed),
        ],
        scratch_shapes=[
            pltpu.VMEM((channels, Q), f32),
            pltpu.VMEM((HP, token_block), f32),
            pltpu.VMEM((own_width, Q), f32),
            pltpu.VMEM((own_width, Q), bf16),
        ],
    )
    found = pl.pallas_call(
        functools.partial(mixer_forward, own_width, heads, kernel_len, places, start, assemble),
        grid_spec=spec,
        out_shape=[
            jax.ShapeDtypeStruct(weight_shape if assemble else (8, Q), bf16),
            jax.ShapeDtypeStruct((places, token_block, model_width), bf16),
            jax.ShapeDtypeStruct((own_width, full), f32),
            jax.ShapeDtypeStruct((channels, full), bf16),
            jax.ShapeDtypeStruct((channels, full), f32),
            jax.ShapeDtypeStruct((own_width, full), bf16),
            jax.ShapeDtypeStruct((3, HP, full), f32),
            jax.ShapeDtypeStruct((full // Q, own_width, Q), bf16),
            jax.ShapeDtypeStruct((channels, Q), bf16),
            jax.ShapeDtypeStruct((own_width, Q), f32),
        ],
        input_output_aliases={
            4 + places + len(weight) + len(carry) + i: 1 + i for i in range(len(written))
        },
        compiler_params=pltpu.CompilerParams(
            dimension_semantics=("arbitrary",), vmem_limit_bytes=48 * MIB
        ),
        cost_estimate=pl.CostEstimate(
            flops=8 * count * token_block * model_width * weight_shape[0],
            bytes_accessed=8 * MIB * count,
            transcendentals=MIB * count,
        ),
        name="mixer_forward",
    )(order, *tokens, gain, chan, head_table, *weight, *carry, *written)
    return found[0] if assemble else weight[0], found[1:8], found[8:]


def run_statistics(order, gates, sent, cotangents, weight, chan):
    places = len(cotangents)
    token_block, model_width = cotangents[0].shape
    own_width, full = gates.shape
    fixed = lambda k, order: (0, 0)
    cols = lambda k, order: (0, k)
    spec = pltpu.PrefetchScalarGridSpec(
        num_scalar_prefetch=1,
        grid=(places,),
        in_specs=[
            pl.BlockSpec((own_width, token_block), cols),
            pl.BlockSpec((own_width, token_block), cols),
            *[pl.BlockSpec((token_block, model_width), fixed)] * places,
            pl.BlockSpec(weight.shape, fixed),
            pl.BlockSpec(chan.shape, fixed),
        ],
        out_specs=[
            pl.BlockSpec((None, token_block, model_width), lambda k, order: (order[k], 0, 0)),
            pl.BlockSpec((own_width, token_block), cols),
            pl.BlockSpec((8, token_block), cols),
        ],
    )
    return pl.pallas_call(
        functools.partial(gate_statistics, places),
        grid_spec=spec,
        out_shape=[
            jax.ShapeDtypeStruct((places, token_block, model_width), bf16),
            jax.ShapeDtypeStruct((own_width, full), f32),
            jax.ShapeDtypeStruct((8, full), f32),
        ],
        compiler_params=pltpu.CompilerParams(
            dimension_semantics=("arbitrary",), vmem_limit_bytes=24 * MIB
        ),
        cost_estimate=pl.CostEstimate(
            flops=2 * full * model_width * own_width,
            bytes_accessed=16 * MIB,
            transcendentals=own_width * full,
        ),
        name="gate_statistics",
    )(order, gates, sent, *cotangents, weight, chan)


def run_gate(order, gates, sent, dbranch, stats, chan, places):
    own_width, full = gates.shape
    token_block = full // places
    cols = lambda k, order: (0, k)
    turned = lambda k, order: (0, order[k])
    spec = pltpu.PrefetchScalarGridSpec(
        num_scalar_prefetch=1,
        grid=(places,),
        in_specs=[
            pl.BlockSpec((own_width, token_block), cols),
            pl.BlockSpec((own_width, token_block), cols),
            pl.BlockSpec((own_width, token_block), cols),
            pl.BlockSpec((8, token_block), cols),
            pl.BlockSpec(chan.shape, lambda k, order: (0, 0)),
        ],
        out_specs=[
            pl.BlockSpec((own_width, token_block), cols),
            pl.BlockSpec((own_width, token_block), turned),
            pl.BlockSpec((own_width, token_block), turned),
        ],
    )
    return pl.pallas_call(
        gate_backward,
        grid_spec=spec,
        out_shape=[jax.ShapeDtypeStruct((own_width, full), bf16)] * 3,
        compiler_params=pltpu.CompilerParams(
            dimension_semantics=("arbitrary",), vmem_limit_bytes=20 * MIB
        ),
        cost_estimate=pl.CostEstimate(
            flops=20 * own_width * full, bytes_accessed=14 * own_width * full, transcendentals=own_width * full
        ),
        name="gate_backward",
    )(order, gates, sent, dbranch, stats, chan)


def run_backward(order, dsent, conv, values, table, states, chan, head_table, heads, kernel_len, places):
    own_width, full = dsent.shape
    channels = chan.shape[0]
    token_block = full // places
    out_rows = channels + HP
    last = places - 1
    fixed = lambda k, order: (0, 0)
    cols = lambda k, order: (0, last - k)
    spec = pltpu.PrefetchScalarGridSpec(
        num_scalar_prefetch=1,
        grid=(places,),
        in_specs=[
            pl.BlockSpec((own_width, token_block), cols),
            pl.BlockSpec((channels, token_block), cols),
            pl.BlockSpec((channels, token_block), cols),
            pl.BlockSpec((3, HP, token_block), lambda k, order: (0, 0, last - k)),
            pl.BlockSpec((token_block // Q, own_width, Q), lambda k, order: (last - k, 0, 0)),
            pl.BlockSpec(chan.shape, fixed),
            pl.BlockSpec(head_table.shape, fixed),
        ],
        out_specs=[
            pl.BlockSpec((out_rows, token_block), lambda k, order: (0, order[last - k])),
            pl.BlockSpec((8, channels), fixed),
            pl.BlockSpec((3, HP, Q), lambda k, order: (0, 0, 0)),
        ],
        scratch_shapes=[
            pltpu.VMEM((kernel_len + 1, channels, Q), f32),
            pltpu.VMEM((own_width, Q), f32),
            pltpu.VMEM((channels, Q), f32),
            pltpu.VMEM((channels, Q), f32),
            pltpu.VMEM((channels, Q), f32),
            pltpu.VMEM((own_width, Q), f32),
            pltpu.VMEM((own_width, Q), f32),
            pltpu.VMEM((own_width, Q), bf16),
            pltpu.VMEM((own_width, Q), bf16),
            pltpu.VMEM((6, HP, Q), f32),
        ],
    )
    return pl.pallas_call(
        functools.partial(mixer_backward, own_width, heads, kernel_len),
        grid_spec=spec,
        out_shape=[
            jax.ShapeDtypeStruct((out_rows, full), bf16),
            jax.ShapeDtypeStruct((8, channels), f32),
            jax.ShapeDtypeStruct((3, HP, Q), f32),
        ],
        compiler_params=pltpu.CompilerParams(
            dimension_semantics=("arbitrary",), vmem_limit_bytes=56 * MIB
        ),
        cost_estimate=pl.CostEstimate(
            flops=32 * MIB * 1024, bytes_accessed=24 * MIB, transcendentals=4 * MIB
        ),
        name="mixer_backward",
    )(order, dsent, conv, values, table, states, chan, head_table)


def token_gradient(dgates_ref, drest_ref, weight_ref, *out_refs):
    own_width = dgates_ref.shape[0]
    total = dot_tn(dgates_ref[...], weight_ref[:own_width, :]) + dot_tn(
        drest_ref[...], weight_ref[own_width:, :]
    )
    for piece, out_ref in enumerate(out_refs):

        @pl.when(pl.program_id(0) == piece)
        def _(out_ref=out_ref):
            out_ref[...] = total.astype(bf16)


def run_token_gradient(dgates, drest, weight, places):
    model_width = weight.shape[1]
    token_block = dgates.shape[1] // places
    fixed = lambda k: (0, 0)
    return pl.pallas_call(
        token_gradient,
        grid=(places,),
        in_specs=[
            pl.BlockSpec((dgates.shape[0], token_block), lambda k: (0, k)),
            pl.BlockSpec((drest.shape[0], token_block), lambda k: (0, k)),
            pl.BlockSpec(weight.shape, fixed),
        ],
        out_specs=[pl.BlockSpec((token_block, model_width), fixed)] * places,
        out_shape=[jax.ShapeDtypeStruct((token_block, model_width), bf16)] * places,
        compiler_params=pltpu.CompilerParams(
            dimension_semantics=("arbitrary",), vmem_limit_bytes=56 * MIB
        ),
        cost_estimate=pl.CostEstimate(
            flops=2 * dgates.shape[1] * weight.size, bytes_accessed=12 * MIB, transcendentals=0
        ),
        name="token_gradient",
    )(dgates, drest, weight)


def weight_gradient(in_rows, core_ref, normed_ref, grad_ref, kept_ref, given_ref):
    total = lax.dot_general(
        normed_ref[...], grad_ref[...], (((0,), (1,)), ((), ())), preferred_element_type=f32
    ).astype(bf16)
    for core in range(2):

        @pl.when(core_ref[0] == core)
        def _(core=core):
            for at in range(kept_ref.shape[0]):
                low = (2 * at + core) * in_rows
                kept_ref[at] = total[low : low + in_rows, :]
                low = (2 * at + 1 - core) * in_rows
                given_ref[at] = total[low : low + in_rows, :]


def run_weight_gradient(core, normed, grad, in_rows, steps):
    full, model_width = normed.shape
    columns = grad.shape[0]
    tile = model_width // steps
    groups = tile // (2 * in_rows)
    spec = pltpu.PrefetchScalarGridSpec(
        num_scalar_prefetch=1,
        grid=(steps,),
        in_specs=[
            pl.BlockSpec((full, tile), lambda k, core: (0, k)),
            pl.BlockSpec(grad.shape, lambda k, core: (0, 0)),
        ],
        out_specs=[pl.BlockSpec((groups, in_rows, columns), lambda k, core: (k, 0, 0))] * 2,
    )
    return pl.pallas_call(
        functools.partial(weight_gradient, in_rows),
        grid_spec=spec,
        out_shape=[jax.ShapeDtypeStruct((groups * steps, in_rows, columns), bf16)] * 2,
        compiler_params=pltpu.CompilerParams(
            dimension_semantics=("arbitrary",), vmem_limit_bytes=56 * MIB
        ),
        cost_estimate=pl.CostEstimate(
            flops=MIB, bytes_accessed=MIB // 8, transcendentals=0
        ),
        name="weight_gradient",
    )(core, normed, grad)


def finish_weight(parts, own_width, state_two, heads, at_in, found_ref, weight_ref, first_ref, second_ref, *outs):
    grad_ref, first_out, second_out, update_out, dot_out = outs
    places = found_ref.shape[0]
    inner = own_width * places
    low = at_in
    for base, total in ((0, inner), (inner, inner), (2 * inner + state_two, heads * places)):
        share = total // (parts * places)
        for part in range(parts):
            for place in range(places):
                to = base + part * (total // parts) + place * share
                grad_ref[:, to : to + share] = found_ref[
                    place, :, low + part * share : low + (part + 1) * share
                ].astype(f32)
        low += total // places
        if base == inner:
            shared = found_ref[0, :, low : low + state_two].astype(f32)
            for place in range(1, places):
                shared = shared + found_ref[place, :, low : low + state_two].astype(f32)
            grad_ref[:, 2 * inner : 2 * inner + state_two] = shared
            low += state_two
    grad = grad_ref[...]
    weight = weight_ref[...].astype(f32)
    _, first_new, second_new, update = adamw(grad, weight, first_ref[...], second_ref[...], 0.1)
    first_out[...] = first_new
    second_out[...] = second_new
    update_out[...] = update
    dot_out[...] = jnp.broadcast_to(jnp.sum(grad * weight, axis=1, keepdims=True), dot_out.shape)


def run_finish(found, weight, first, second, parts, own_width, state_two, heads, at_in):
    rows, columns = weight.shape
    step = 16 if rows % 16 == 0 else rows
    whole = pl.BlockSpec((step, columns), lambda k: (k, 0))
    return pl.pallas_call(
        functools.partial(finish_weight, parts, own_width, state_two, heads, at_in),
        grid=(rows // step,),
        in_specs=[
            pl.BlockSpec((found.shape[0], step, found.shape[2]), lambda k: (0, k, 0)),
            whole,
            whole,
            whole,
        ],
        out_specs=[whole] * 4 + [pl.BlockSpec((step, Q), lambda k: (k, 0))],
        out_shape=[jax.ShapeDtypeStruct((rows, columns), f32)] * 4
        + [jax.ShapeDtypeStruct((rows, Q), f32)],
        compiler_params=pltpu.CompilerParams(
            dimension_semantics=("arbitrary",), vmem_limit_bytes=32 * MIB
        ),
        cost_estimate=pl.CostEstimate(
            flops=20 * rows * columns, bytes_accessed=28 * rows * columns, transcendentals=rows * columns
        ),
        name="finish_weight",
    )(found, weight, first, second)


def adamw(grad, weight, first, second, decay):
    first_new = beta_one * first + (1.0 - beta_one) * grad
    second_new = beta_two * second + (1.0 - beta_two) * grad * grad
    update = -learn_rate * (
        first_new / first_fix / (jnp.sqrt(second_new / second_fix) + adam_eps) + decay * weight
    )
    return (grad, first_new, second_new, update)


def pieces_for(stacked, index):
    return lax.dynamic_index_in_dim(stacked, index, 0, keepdims=False)


def local(
    block_input,
    cotangent,
    norm_gain,
    norm_mean,
    norm_square,
    inproj_weight,
    inproj_mean,
    inproj_square,
    conv_params,
    conv_mean,
    conv_square,
    head_params,
    head_mean,
    head_square,
    gate_gain,
    gate_mean,
    gate_square,
    outproj_weight,
    outproj_mean,
    outproj_square,
):
    group = lax.axis_size("seq")
    shards = lax.axis_size("wshard")
    seq_index = lax.axis_index("seq")
    shard = lax.axis_index("wshard")
    places = group // 2
    place = seq_index // 2
    core = seq_index % 2
    sequences, local_len, model_width = block_input.shape
    inner_width = gate_gain.shape[0] * shards
    head_count = head_params.shape[1] * shards
    kernel_len = conv_params.shape[0] - 1
    state_two = conv_params.shape[1] * shards - inner_width
    if sequences != 2 or places != shards or state_two != 2 * Q:
        raise ValueError("unexpected sizes")
    own_width = inner_width // places
    heads = head_count // places
    width = inner_width // head_count

    parts = shards if head_count % (shards * places) == 0 else 1

    def own_part(x, axis):
        size = x.shape[axis]
        share = size // (parts * places)
        return jnp.concatenate(
            [
                lax.dynamic_slice_in_dim(x, i * (size // parts) + place * share, share, axis)
                for i in range(parts)
            ],
            axis=axis,
        )

    def whole(x):
        x = x.reshape(x.shape[:-1] + (parts, -1))
        x = jnp.moveaxis(x, 0, -2)
        return x.reshape(x.shape[:-3] + (-1,))

    def swap(x):
        return lax.ppermute(x, "seq", [(i, i ^ 1) for i in range(group)])

    def along(x, mask, among=None):
        pairs = [(i, i ^ (2 * mask)) for i in range(group)]
        if among is not None:
            pairs = [(a, b) for a, b in pairs if b // 2 in among]
        return lax.ppermute(x, "seq", pairs)

    def across(x, mask):
        return lax.ppermute(x, "wshard", [(i, i ^ mask) for i in range(shards)])

    def shard_exchange(x):
        return lax.all_to_all(x, "wshard", split_axis=0, concat_axis=0, tiled=True)

    def shard_gather(x):
        return shard_exchange(jnp.broadcast_to(x[None], (shards,) + x.shape))

    def line_exchange(x):
        groups = [[2 * i + c for i in range(places)] for c in range(2)]
        return lax.all_to_all(
            x, "seq", split_axis=0, concat_axis=0, tiled=True, axis_index_groups=groups
        )

    small = jnp.concatenate(
        [norm_gain, gate_gain, conv_params.reshape(-1), head_params.reshape(-1)]
    )
    tokens = block_input.astype(f32)
    scale = lax.rsqrt(jnp.mean(tokens * tokens, axis=-1, keepdims=True) + norm_eps)

    def join(kept, other):
        return jnp.where(core == 0, jnp.concatenate([kept, other]), jnp.concatenate([other, kept]))

    def to_sequence(x):
        kept = lax.dynamic_index_in_dim(x, core, 0, keepdims=False)
        other = swap(lax.dynamic_index_in_dim(x, 1 - core, 0, keepdims=False))
        return join(kept, other)

    def to_tokens(x):
        halves = x.reshape(2, local_len, -1)
        kept = lax.dynamic_index_in_dim(halves, core, 0, keepdims=True)
        other = swap(lax.dynamic_index_in_dim(halves, 1 - core, 0, keepdims=True))
        return join(kept, other)

    def gather_first(x):
        return [along(x, mask) for mask in range(1, 3 if places == 4 else places)]

    def gather_last(x, first):
        return [along(x, 3, (1, 2)), along(first[1], 1, (0, 3))] if places == 4 else []

    def gathered(x, first, last):
        if places != 4:
            return [x] + first
        return [x] + first + [jnp.where((place == 0) | (place == 3), last[1], last[0])]

    def scatter_first(pieces):
        if places != 4:
            return []
        return [along(pieces[3], 1, (1, 2)), along(pieces[3], 3, (1, 2))]

    def scatter_second(pieces, first):
        if places != 4:
            return [pieces[0]] + [along(pieces[mask], mask) for mask in range(1, places)]
        far = (pieces[2].astype(f32) + first[0].astype(f32)).astype(pieces[2].dtype)
        return [pieces[0], along(pieces[1], 1), along(far, 2), first[1]]

    def in_order(found):
        stacked = jnp.stack(found)
        return jnp.stack([pieces_for(stacked, place ^ k) for k in range(places)])

    order = jnp.concatenate(
        [jnp.arange(places, dtype=jnp.int32) ^ place, core.reshape(1).astype(jnp.int32)]
    )
    token_own = to_sequence(block_input)

    half_cols = jnp.concatenate(
        [
            own_part(
                lax.dynamic_slice_in_dim(inproj_weight, core * inner_width, inner_width, 1), 1
            ),
            lax.dynamic_slice_in_dim(inproj_weight, 2 * inner_width + core * Q, Q, 1),
            jnp.pad(
                own_part(inproj_weight[:, 2 * inner_width + state_two :], 1),
                ((0, 0), (0, HP - heads)),
            ),
        ],
        axis=1,
    ).T
    shard_rows = half_cols.shape[1]
    small_rows = -(-small.shape[0] // (16 * shard_rows)) * 16
    small_pad = jnp.pad(small, (0, small_rows * shard_rows - small.shape[0]))
    sending = jnp.concatenate([half_cols, small_pad.reshape(small_rows, shard_rows)])
    sending = jnp.broadcast_to(sending[None], (shards,) + sending.shape)
    cot_own = to_sequence(cotangent)
    token_own, sending = lax.optimization_barrier((token_own, sending))
    token_first = gather_first(token_own)
    found = shard_exchange(sending)
    token_own, found, cot_own, outproj_late, *token_first = lax.optimization_barrier(
        (token_own, found, cot_own, outproj_weight, *token_first)
    )
    small_all = found[:, half_cols.shape[0] :].reshape(shards, -1)
    at_gate = norm_gain.shape[0]
    at_conv = at_gate + gate_gain.shape[0]
    at_head = at_conv + conv_params.size
    gain_f = small_all[:, :at_gate].reshape(-1).astype(f32)
    gate_f = small_all[:, at_gate:at_conv].reshape(-1).astype(f32)
    conv_f = (
        small_all[:, at_conv:at_head]
        .reshape(shards, kernel_len + 1, -1)
        .transpose(1, 0, 2)
        .reshape(kernel_len + 1, -1)
        .astype(f32)
    )
    head_f = (
        small_all[:, at_head : small.shape[0]].reshape(shards, 3, -1).transpose(1, 0, 2).reshape(3, -1).astype(f32)
    )
    taps = jnp.concatenate(
        [
            own_part(conv_f[:, :inner_width], 1),
            conv_f[:, inner_width:],
        ],
        axis=1,
    )
    channels = taps.shape[1]
    head_own = own_part(head_f, 1)
    gate_own = own_part(gate_f, 0)
    skip_gain = jnp.pad(
        jnp.stack([jnp.repeat(head_own[2], width), gate_own]), ((0, 0), (0, state_two))
    )
    chan = jnp.concatenate(
        [taps, jnp.zeros((6 - taps.shape[0], channels), f32), skip_gain], axis=0
    ).T
    rates = -jnp.exp(head_own[0])
    head_table = jnp.pad(
        jnp.stack([rates, head_own[1]], axis=1), ((0, HP - heads), (0, Q - 2))
    )

    token_last = gather_last(token_own, token_first)
    cot_first = gather_first(cot_own)
    half_width = model_width // 2
    share = own_width // parts
    out_sending = [lax.dynamic_slice_in_dim(outproj_late, core * half_width, half_width, 1)]
    if parts == shards:
        out_sending = [
            lax.dynamic_slice_in_dim(outproj_late, place * share, share, 0)
        ] + out_sending
    out_sending = [jnp.broadcast_to(x[None], (shards,) + x.shape) for x in out_sending]
    out_found = shard_exchange(out_sending[0])
    token_own, token_first, token_last, cot_own, cot_first, out_found = lax.optimization_barrier(
        (token_own, token_first, token_last, cot_own, cot_first, out_found)
    )
    token_pieces = gathered(token_own, token_first, token_last)
    other_found = swap(found)
    if shard_rows % Q == 0:
        weight = [found, other_found]
    else:
        turned = lambda x: x[:, : half_cols.shape[0]].transpose(1, 0, 2).reshape(-1, model_width)
        own_half, other_half = turned(found), turned(other_found)
        first = jnp.where(core == 0, own_half, other_half)
        second = jnp.where(core == 0, other_half, own_half)
        weight = [
            jnp.concatenate(
                [
                    first[:own_width],
                    second[:own_width],
                    first[own_width : own_width + Q],
                    second[own_width : own_width + Q],
                    own_half[own_width + Q :],
                ]
            )
        ]
    out_half = shard_exchange(out_sending[1]) if parts == shards else out_found
    def whole_columns(own, other):
        return jnp.where(
            core == 0, jnp.concatenate([own, other], axis=1), jnp.concatenate([other, own], axis=1)
        )

    def own_piece(param, count, axis_dim):
        return lax.dynamic_slice_in_dim(param, seq_index * count, count, axis_dim)

    def own_rows(x):
        return own_part(x, 0)


    forward = functools.partial(
        run_forward, order, token_pieces, gain_f[None], chan, head_table, own_width, heads, kernel_len
    )
    weight, written, carry = forward(0, places, weight, [], [])
    inproj_own = own_piece(inproj_weight, inproj_mean.shape[0], 0)
    cot_last = gather_last(cot_own, cot_first)
    written, inproj_own, cot_own, cot_first, cot_last = lax.optimization_barrier(
        (written, inproj_own, cot_own, cot_first, cot_last)
    )
    cot_pieces = gathered(cot_own, cot_first, cot_last)
    if parts == shards:
        outproj_own = out_found.reshape(own_width, model_width)
    else:
        out_rows_own = lax.optimization_barrier(own_rows(out_found.reshape(inner_width, half_width)))
        outproj_own = whole_columns(out_rows_own, swap(out_rows_own))
    normed_all, gates, values, conv, sent, table, states = written
    cot_all, dbranch, stat = run_statistics(order, gates, sent, cot_pieces, outproj_own, chan)
    stat = stat[:2]
    stat = stat + sum(along(stat, mask) for mask in range(1, places))
    grms = lax.rsqrt(stat[0] / inner_width + norm_eps)
    stats = jnp.pad(
        jnp.stack([grms, grms * grms * (stat[1] / inner_width)]), ((0, 6), (0, 0))
    )
    dsent, dgates, branch = run_gate(order, gates, sent, dbranch, stats, chan, places)
    dsent, dgates, branch, out_half = lax.optimization_barrier((dsent, dgates, branch, out_half))
    token_block = 2 * local_len
    flat = places * token_block

    def columns(x, m):
        return x[:, m * token_block : (m + 1) * token_block]

    token_block = 2 * local_len
    flat = places * token_block

    def columns(x, m):
        return x[:, m * token_block : (m + 1) * token_block]

    def over_cores(x, axis):
        kept = lax.dynamic_index_in_dim(x, core, axis, keepdims=False)
        other = lax.dynamic_index_in_dim(x, 1 - core, axis, keepdims=False)
        return kept, other

    def added(kept, other):
        return (kept.astype(f32) + other.astype(f32)).astype(bf16)

    in_rows = inproj_mean.shape[0]
    out_rows = outproj_mean.shape[0]

    def inproj_local(grad_rows):
        normed_flat = normed_all.reshape(flat, model_width)
        shape = (shards, places, in_rows, grad_rows.shape[0])
        if in_rows % 16 == 0:
            steps = min(shards, model_width // Q)
            kept, given = run_weight_gradient(
                core.reshape(1).astype(jnp.int32), normed_flat, grad_rows, in_rows, steps
            )
            return kept.reshape(shape), given.reshape(shape)
        part = lax.dot_general(
            normed_flat, grad_rows, (((0,), (1,)), ((), ())), preferred_element_type=f32
        ).astype(bf16)
        return over_cores(part.reshape(shards, places, 2, in_rows, -1), 2)

    branch_found = [along(columns(branch, m), m) for m in range(1, places)]
    out_part = jnp.dot(branch, cot_all.reshape(flat, model_width), preferred_element_type=f32).astype(bf16)
    out_kept, out_part = over_cores(out_part.reshape(shards, 2, out_rows, model_width), 1)
    out_part = swap(out_part)
    gate_kept, gate_part = inproj_local(dgates)
    gate_part = swap(gate_part)
    dsent, out_kept, gate_kept = lax.optimization_barrier((dsent, out_kept, gate_kept))
    drest, conv_sums, head_acc = run_backward(
        order, dsent, conv, values, table, states, chan, head_table, heads, kernel_len, places
    )
    rest_kept, rest_part = inproj_local(drest)
    rest_part = swap(rest_part)
    drest, rest_kept, branch_found, out_part, gate_part, conv_sums, head_acc, out_half = (
        lax.optimization_barrier(
            (drest, rest_kept, branch_found, out_part, gate_part, conv_sums, head_acc, out_half)
        )
    )
    out_half = out_half.reshape(inner_width, half_width)
    out_other = swap(out_half)
    head_sums = jnp.sum(head_acc, axis=-1)[:, :heads]
    head_sums = jnp.concatenate([head_sums[:1] * rates, head_sums[1:]])
    conv_sums = conv_sums[: kernel_len + 1]
    sums = jnp.concatenate([conv_sums.reshape(-1), head_sums.reshape(-1)])
    sums = sums + swap(sums)
    out_sum = added(out_kept, out_part)
    out_sum = jnp.concatenate(
        [out_sum[:, :, i : i + own_width] for i in range(0, model_width, own_width)], axis=1
    ).reshape(shards, places * in_rows, -1)
    gate_sum = added(gate_kept, gate_part).reshape(shards, places * in_rows, -1)
    drest, out_sum, gate_sum = lax.optimization_barrier((drest, out_sum, gate_sum))
    dn_pieces = run_token_gradient(dgates, drest, weight, places)
    sums, rest_part, out_other, *dn_pieces = lax.optimization_barrier(
        (sums, rest_part, out_other, *dn_pieces)
    )
    dn_first = scatter_first(dn_pieces)
    def halves(x, rows):
        high = lax.reduce_precision(x, 8, 7)
        both = jnp.concatenate([high, x - high]).astype(bf16)
        across_rows = -(-both.shape[0] // (rows * Q)) * Q
        return jnp.pad(both, (0, rows * across_rows - both.shape[0])).reshape(rows, across_rows)

    def joined_halves(x, count):
        x = x.reshape(x.shape[:-2] + (-1,))
        return x[..., :count] + x[..., count : 2 * count]

    small_sums = halves(sums, places * in_rows)
    joined = jnp.concatenate(
        [
            jnp.broadcast_to(small_sums[None], (shards,) + small_sums.shape),
            out_sum,
            gate_sum,
            added(rest_kept, rest_part).reshape(shards, places * in_rows, -1),
        ],
        axis=2,
    )
    joined = shard_exchange(joined)
    dn_pieces, dn_first = lax.optimization_barrier((dn_pieces, dn_first))
    dn_found = scatter_second(dn_pieces, dn_first)
    dn_found[1], branch_found, branch = lax.optimization_barrier((dn_found[1], branch_found, branch))
    branch_all = in_order([columns(branch, 0)] + branch_found)
    branch_all = branch_all.reshape(places, parts, -1, token_block).swapaxes(0, 1)
    branch_all = branch_all.reshape(inner_width, token_block)
    out = whole_columns(dot_tn(branch_all, out_half), dot_tn(branch_all, out_other))
    out, joined, dn_found = lax.optimization_barrier((out, joined, dn_found))
    joined = jnp.sum(joined.astype(f32), axis=0)
    at_out = small_sums.shape[1]
    at_in = at_out + out_rows * model_width // (places * in_rows)
    small_sums = halves(joined_halves(joined[:, :at_out], sums.shape[0]), in_rows)
    rest_side = jnp.concatenate(
        [
            jnp.broadcast_to(small_sums[None], (places,) + small_sums.shape),
            joined[:, at_in:].reshape(places, in_rows, -1).astype(bf16),
        ],
        axis=2,
    )
    rest_side, dn_found, out = lax.optimization_barrier((rest_side, dn_found, out))
    rest_side = line_exchange(rest_side)
    outproj_grad = joined[:, at_out:at_in].reshape(-1, out_rows, own_width)
    outproj_grad = outproj_grad.swapaxes(0, 1).reshape(out_rows, model_width)
    if parts == 1:
        outproj_grad = lax.ppermute(
            outproj_grad,
            ("wshard", "seq"),
            [
                (a * group + 2 * b + c, b * group + 2 * a + c)
                for a in range(shards)
                for b in range(places)
                for c in range(2)
            ],
        )

    at_in = small_sums.shape[1]
    lines = joined_halves(rest_side[:, :, :at_in].astype(f32), sums.shape[0])
    conv_lines = lines[:, : conv_sums.size].reshape(places, kernel_len + 1, channels)
    conv_total = jnp.concatenate(
        [
            whole(conv_lines[:, :, :own_width]),
            jnp.sum(conv_lines[:, :, own_width:], axis=0),
        ],
        axis=1,
    )
    head_total = whole(lines[:, conv_sums.size :].reshape(places, 3, heads))
    block_output = tokens + to_tokens(out)
    dnormed = sum(piece.astype(f32) for piece in dn_found)
    dn_scaled = to_tokens(dnormed) * gain_f
    input_grad = (
        cotangent.astype(f32)
        + scale * dn_scaled
        - tokens * scale * scale * scale * jnp.mean(dn_scaled * tokens, axis=-1, keepdims=True)
    )

    inproj_grad, *inproj_new, inproj_dot = run_finish(
        rest_side, inproj_own, inproj_mean, inproj_square, parts, own_width, state_two, heads, at_in
    )
    inproj_res = (inproj_grad, *inproj_new)
    conv_width = conv_mean.shape[1]
    conv_grad = lax.dynamic_slice_in_dim(
        conv_total, (shard * group + seq_index) * conv_width, conv_width, 1
    )
    head_width = head_params.shape[1]
    head_grad = lax.dynamic_slice_in_dim(head_total, shard * head_width, head_width, 1)

    outproj_piece = own_piece(outproj_weight, out_rows, 0).astype(f32)
    norm_own = own_piece(norm_gain, in_rows, 0).astype(f32)
    gate_piece = own_piece(gate_gain, out_rows, 0).astype(f32)
    norm_grad = inproj_dot[:, 0] / norm_own
    gate_grad = jnp.sum(outproj_piece * outproj_grad, axis=1) / gate_piece
    norm_res = adamw(norm_grad, norm_own, norm_mean, norm_square, 0.0)
    conv_res = adamw(conv_grad, own_piece(conv_params, conv_width, 1).astype(f32), conv_mean, conv_square, 0.0)
    head_res = adamw(head_grad, head_params.astype(f32), head_mean, head_square, 0.0)
    gate_res = adamw(gate_grad, gate_piece, gate_mean, gate_square, 0.0)
    outproj_res = adamw(outproj_grad, outproj_piece, outproj_mean, outproj_square, 0.1)
    return (
        block_output,
        input_grad,
        norm_res[0],
        norm_res[1],
        norm_res[2],
        norm_res[3],
        inproj_res[0],
        inproj_res[1],
        inproj_res[2],
        inproj_res[3],
        conv_res[0],
        conv_res[1],
        conv_res[2],
        conv_res[3],
        head_res[0],
        head_res[1],
        head_res[2],
        head_res[3],
        gate_res[0],
        gate_res[1],
        gate_res[2],
        gate_res[3],
        outproj_res[0],
        outproj_res[1],
        outproj_res[2],
        outproj_res[3],
    )


def solution(mesh):
    placed = (
        P("wshard", "seq", None),
        P("wshard", "seq", None),
        P("wshard"),
        P(("wshard", "seq")),
        P(("wshard", "seq")),
        P("wshard", None),
        P(("wshard", "seq"), None),
        P(("wshard", "seq"), None),
        P(None, "wshard"),
        P(None, ("wshard", "seq")),
        P(None, ("wshard", "seq")),
        P(None, "wshard"),
        P(None, "wshard"),
        P(None, "wshard"),
        P("wshard"),
        P(("wshard", "seq")),
        P(("wshard", "seq")),
        P("wshard", None),
        P(("wshard", "seq"), None),
        P(("wshard", "seq"), None),
    )
    return jax.shard_map(
        local,
        mesh=mesh,
        in_specs=placed,
        out_specs=(
            P("wshard", "seq", None),
            P("wshard", "seq", None),
            P(("wshard", "seq")),
            P(("wshard", "seq")),
            P(("wshard", "seq")),
            P(("wshard", "seq")),
            P(("wshard", "seq"), None),
            P(("wshard", "seq"), None),
            P(("wshard", "seq"), None),
            P(("wshard", "seq"), None),
            P(None, ("wshard", "seq")),
            P(None, ("wshard", "seq")),
            P(None, ("wshard", "seq")),
            P(None, ("wshard", "seq")),
            P(None, "wshard"),
            P(None, "wshard"),
            P(None, "wshard"),
            P(None, "wshard"),
            P(("wshard", "seq")),
            P(("wshard", "seq")),
            P(("wshard", "seq")),
            P(("wshard", "seq")),
            P(("wshard", "seq"), None),
            P(("wshard", "seq"), None),
            P(("wshard", "seq"), None),
            P(("wshard", "seq"), None),
        ),
        check_vma=False,
    )
```

profile of v0, /device:TPU:0, one launch (start us, length us, event | category | flops | bytes accessed | tf_op | source)
XLA Modules:
  0.0 341.4 jit_solution(15060407323310913194)
XLA Ops:
  0.8 1.2 dynamic-slice_bitcast_fusion.5
  5.4 1.0 dynamic-slice_dynamic-update-slice_fusion
  8.0 1.8 broadcast_in_dim.18
  9.8 4.9 %all-to-all-start = ((bf16[4,928,384]{2,1,0:T(8,128)(2,1)}), bf16[4,928,384]{2,1,0:T(8,128)(2,1)}, u32[]{:S(2)}, u32[]{:S(2)}) async-start(bf16[4,928,384]{2,1,0:T(8,128)(2,1)} %broadcast_in_dim.18), calls=%async_computation | async-start | bytes 5701632 | tf_op jit(solution)/shard_map/all_to_all | solution.py:815
  15.7 2.8 collective-permute-start.2
  18.4 2.6 collective-permute-start.3
  21.0 3.7 %constant_dynamic-slice_fusion.11 = bf16[48,6448]{0,1:T(8,128)(2,1)} fusion(bf16[384,6448]{0,1:T(8,128)(2,1)} %param.25, s32[]{:T(128)S(6)} %select_n.182), kind=kLoop, calls=%fused_computation.101 | loop fusion | bytes 1238020 | tf_op jit(solution)/shard_map/dynamic_slice | solution.py:980
  24.7 1.8 copy.93.weight_ref
  26.7 2.2 maximum_select_fusion.4.refs_0_
  29.0 24.0 %collective-permute-done.2.refs_1_ = bf16[256,1536]{1,0:T(8,128)(2,1)S(1)} collective-permute-done((bf16[256,1536]{1,0:T(8,128)(2,1)S(1)}, bf16[256,1536]{1,0:T(8,128)(2,1)S(1)}, u32[]{:S(2)}, u32[]{:S(2)}) %collective-permute-start.2) | collective-permute-done | bytes 786464 | tf_op jit(solution)/shard_map/ppermute | solution.py:809
  52.9 2.5 collective-permute-done.3.refs_2_
  57.1 2.6 collective-permute-start.7
  60.0 1.1 constant_dynamic-slice_fusion.20
  61.1 1.6 broadcast_in_dim.19
  62.7 4.1 %all-to-all-start.1 = ((bf16[4,192,1536]{2,1,0:T(8,128)(2,1)}), bf16[4,192,1536]{2,1,0:T(8,128)(2,1)S(1)}, u32[]{:S(2)}, u32[]{:S(2)}) async-start(bf16[4,192,1536]{2,1,0:T(8,128)(2,1)} %broadcast_in_dim.19), calls=%async_computation.1 | async-start | bytes 4718592 | tf_op jit(solution)/shard_map/all_to_all | solution.py:815
  67.4 1.5 collective-permute-start.4
  69.0 1.3 collective-permute-start.5
  72.8 2.4 constant_dynamic-slice_fusion.10
  75.2 19.4 %all-to-all-done.1 = bf16[4,192,1536]{2,1,0:T(8,128)(2,1)S(1)} async-done(((bf16[4,192,1536]{2,1,0:T(8,128)(2,1)}), bf16[4,192,1536]{2,1,0:T(8,128)(2,1)S(1)}, u32[]{:S(2)}, u32[]{:S(2)}) %all-to-all-start.1) | async-done | bytes 2359328 | tf_op jit(solution)/shard_map/all_to_all | solution.py:815
  94.6 3.7 %broadcast_in_dim.22 = bf16[4,768,768]{2,1,0:T(8,128)(2,1)} broadcast(bf16[768,768]{1,0:T(8,128)(2,1)} %constant_dynamic-slice_fusion.10), dimensions={1,2} | broadcast | bytes 5898240 | tf_op jit(solution)/shard_map/broadcast_in_dim | solution.py:948
  98.3 5.0 %all-to-all-start.2 = ((bf16[4,768,768]{2,1,0:T(8,128)(2,1)}), bf16[4,768,768]{2,1,0:T(8,128)(2,1)}, u32[]{:S(2)}, u32[]{:S(2)}) async-start(bf16[4,768,768]{2,1,0:T(8,128)(2,1)} %broadcast_in_dim.22), calls=%async_computation.2 | async-start | bytes 9437184 | tf_op jit(solution)/shard_map/all_to_all | solution.py:815
  103.3 7.4 %collective-permute-done.5 = bf16[256,1536]{1,0:T(8,128)(2,1)} collective-permute-done((bf16[256,1536]{1,0:T(8,128)(2,1)}, bf16[256,1536]{1,0:T(8,128)(2,1)}, u32[]{:S(2)}, u32[]{:S(2)}) %collective-permute-start.5) | collective-permute-done | bytes 786464 | tf_op jit(solution)/shard_map/ppermute | solution.py:809
  110.7 1.3 collective-permute-start.10
  112.9 1.2 broadcast_select_fusion.1.refs_3_
  114.1 27.4 %mixer_forward.1 = (bf16[1808,1536]{1,0:T(8,128)(2,1)}, bf16[4,256,1536]{2,1,0:T(8,128)(2,1)}, f32[768,1024]{1,0:T(8,128)}, bf16[1024,1024]{1,0:T(8,128)(2,1)}, ...) custom-call(s32[5]{0:T(128)S(1)} %pad_add_fusion.order_ref, ...), custom_call_target="tpu_custom_call" | custom-call | flops 22749904896 | bytes 33554432 | tf_op jit(solution)/shard_map/mixer_forward/pallas_call | solution.py:433
  142.3 1.9 copy-done
  144.1 7.1 %gate_statistics.1 = (bf16[4,256,1536]{2,1,0:T(8,128)(2,1)S(1)}, f32[768,1024]{1,0:T(8,128)S(1)}, f32[8,1024]{1,0:T(8,128)S(1)}) custom-call(s32[5]{0:T(128)S(1)} %pad_add_fusion.order_ref, f32[768,1024]{1,0:T(8,128)S(1)} %copy-done, bf16[768,1024]{1,0:T(8,128)(2,1)S(1)} %get-tuple-element.159.sent_ref, bf16[256,1536]{1,0:T(8,128)(2,1)} %maximum_select_fusion.4.refs_0_, ...), custom_call_target="tpu_custom_call" | custom-call | flops 2415919104 | bytes 16777216 | tf_op jit(solution)/shard_map/gate_statistics/pallas_call | solution.py:486
  151.2 1.7 copy-done.10
  153.0 5.5 %collective-permute-start.11 = (f32[2,1024]{1,0:T(2,128)S(1)}, f32[2,1024]{1,0:T(2,128)S(1)}, u32[]{:S(2)}, u32[]{:S(2)}) collective-permute-start(f32[2,1024]{1,0:T(2,128)S(1)} %slice.123), channel_id=1, source_target_pairs={{0,2},{1,3},{2,0},{3,1},{4,6},{5,7},{6,4},{7,5},{8,10},{9,11},{10,... | collective-permute-start | bytes 24584 | tf_op jit(solution)/shard_map/ppermute | solution.py:809
  158.4 2.4 collective-permute-start.13
  160.8 2.2 collective-permute-done.12
  164.0 4.5 %gate_backward.1 = (bf16[768,1024]{1,0:T(8,128)(2,1)S(1)}, bf16[768,1024]{1,0:T(8,128)(2,1)S(1)}, bf16[768,1024]{1,0:T(8,128)(2,1)S(1)}) custom-call(s32[5]{0:T(128)S(1)} %pad_add_fusion.order_ref, f32[768,1024]{1,0:T(8,128)S(1)} %copy-done.1, bf16[768,1024]{1,0:T(8,128)(2,1)S(1)} %get-tuple-element.159.sent_ref, ...), custom_call_target="tpu_custom_call" | custom-call | flops 15728640 | bytes 11010048 | tf_op jit(solution)/shard_map/gate_backward/pallas_call | solution.py:527
  168.5 1.1 copy-done.3
  169.6 1.1 copy-done.11
  170.8 1.1 fusion.44
  171.8 4.7 %convolution_convert_fusion = bf16[768,1536]{1,0:T(8,128)(2,1)S(1)} fusion(bf16[768,1024]{1,0:T(8,128)(2,1)S(1)} %get-tuple-element.211, bf16[1024,1536]{1,0:T(8,128)(2,1)} %bitcast.82), kind=kOutput, calls=%fused_computation.3 | convolution fusion | flops 2417098752 | bytes 7077888 | tf_op jit(solution)/shard_map/dot_general | solution.py:1049
  176.7 6.6 %weight_gradient.2 = (bf16[16,48,768]{2,1,0:T(8,128)(2,1)}, bf16[16,48,768]{2,1,0:T(8,128)(2,1)}) custom-call(s32[1]{0:T(128)} %bitcast.core_ref, bf16[1024,1536]{1,0:T(8,128)(2,1)} %bitcast.83, bf16[768,1024]{1,0:T(8,128)(2,1)} %copy-done.3), custom_call_target="tpu_custom_call" | custom-call | flops 1048576 | bytes 131072 | tf_op jit(solution)/shard_map/weight_gradient/pallas_call | solution.py:662
  183.9 2.8 collective-permute-start.15
  186.7 1.5 collective-permute-start.16
  188.2 26.0 %mixer_backward.1 = (bf16[1040,1024]{1,0:T(8,128)(2,1)}, f32[8,1024]{1,0:T(8,128)}, f32[3,16,128]{2,1,0:T(8,128)}) custom-call(s32[5]{0:T(128)} %copy-done.9, bf16[768,1024]{1,0:T(8,128)(2,1)} %copy-done.11, f32[1024,1024]{1,0:T(8,128)} %get-tuple-element.178.conv_ref, bf16[1024,1024]{1,0:T(8,128)(2,1)} %get-tuple-element.179.values_ref, ...), custom_call_target="tpu_custom_call" | custom-call | flops 34359738368 | bytes 25165824 | tf_op jit(solution)/shard_map/mixer_backward/pallas_call | solution.py:579
  214.2 8.3 %weight_gradient.3 = (bf16[16,48,1040]{2,1,0:T(8,128)(2,1)}, bf16[16,48,1040]{2,1,0:T(8,128)(2,1)}) custom-call(s32[1]{0:T(128)} %bitcast.core_ref, bf16[1024,1536]{1,0:T(8,128)(2,1)} %bitcast.84, bf16[1040,1024]{1,0:T(8,128)(2,1)} %get-tuple-element.197.grad_ref.drest_ref), custom_call_target="tpu_custom_call" | custom-call | flops 1048576 | bytes 131072 | tf_op jit(solution)/shard_map/weight_gradient/pallas_call | solution.py:662
  224.1 1.1 pad_maximum_fusion.3
  228.4 12.3 %token_gradient.1 = (bf16[256,1536]{1,0:T(8,128)(2,1)}, bf16[256,1536]{1,0:T(8,128)(2,1)}, bf16[256,1536]{1,0:T(8,128)(2,1)}, bf16[256,1536]{1,0:T(8,128)(2,1)}) custom-call(bf16[768,1024]{1,0:T(8,128)(2,1)} %copy-done.3, bf16[1040,1024]{1,0:T(8,128)(2,1)} %get-tuple-element.197.grad_ref.drest_ref, bf16[1808,1536]{1,0:T(8,128)(2,1)} %get-tuple-element.198.weight_ref), custom_call_target="tpu_custom_call" | custom-call | flops 5687476224 | bytes 12582912 | tf_op jit(solution)/shard_map/token_gradient/pallas_call | solution.py:613
  240.7 2.2 collective-permute-start.22
  243.0 1.6 collective-permute-start.23
  244.6 2.0 add_convert_fusion
  246.7 2.2 pad_maximum_fusion
  248.9 5.1 %all-to-all-start.3 = ((bf16[4,192,2704]{2,1,0:T(8,128)(2,1)}), bf16[4,192,2704]{2,1,0:T(8,128)(2,1)}, u32[]{:S(2)}, u32[]{:S(2)}) async-start(bf16[4,192,2704]{2,1,0:T(8,128)(2,1)} %pad_maximum_fusion), calls=%async_computation.3 | async-start | bytes 8650752 | tf_op jit(solution)/shard_map/all_to_all | solution.py:815
  254.0 5.6 %collective-permute-done.22 = bf16[256,1536]{1,0:T(8,128)(2,1)} collective-permute-done((bf16[256,1536]{1,0:T(8,128)(2,1)}, bf16[256,1536]{1,0:T(8,128)(2,1)}, u32[]{:S(2)}, u32[]{:S(2)}) %collective-permute-start.22) | collective-permute-done | bytes 786464 | tf_op jit(solution)/shard_map/ppermute | solution.py:809
  259.6 3.4 collective-permute-start.24
  263.0 1.7 add_convert_fusion.3
  264.7 1.0 collective-permute-start.25
  265.7 29.5 %collective-permute-done.24 = bf16[256,1536]{1,0:T(8,128)(2,1)S(1)} collective-permute-done((bf16[256,1536]{1,0:T(8,128)(2,1)}, bf16[256,1536]{1,0:T(8,128)(2,1)S(1)}, u32[]{:S(2)}, u32[]{:S(2)}) %collective-permute-start.24) | collective-permute-done | bytes 786464 | tf_op jit(solution)/shard_map/ppermute | solution.py:809
  296.6 3.8 %fusion.47 = f32[256,768]{1,0:T(8,128)S(1)} fusion(bf16[3072,256]{1,0:T(8,128)(2,1)S(1)} %bitcast.97, bf16[3072,768]{1,0:T(8,128)(2,1)} %bitcast.22), kind=kOutput, calls=%fused_computation.162 | convolution fusion | flops 1207959552 | bytes 7077888 | tf_op jit(solution)/shard_map/dot_general | solution.py:35
  300.3 3.8 %fusion.48 = f32[256,768]{1,0:T(8,128)S(1)} fusion(bf16[3072,256]{1,0:T(8,128)(2,1)S(1)} %bitcast.98, bf16[3072,768]{1,0:T(8,128)(2,1)} %collective-permute-done.21), kind=kOutput, calls=%fused_computation.163 | convolution fusion | flops 1207959552 | bytes 7077888 | tf_op jit(solution)/shard_map/dot_general | solution.py:35
  304.3 3.1 convert_reduce_fusion
  309.5 3.5 %all-to-all-start.4 = ((bf16[4,48,2064]{2,1,0:T(8,128)(2,1)}), bf16[4,48,2064]{2,1,0:T(8,128)(2,1)S(1)}, u32[]{:S(2)}, u32[]{:S(2)}) async-start(bf16[4,48,2064]{2,1,0:T(8,128)(2,1)} %pad_maximum_fusion.4), calls=%async_computation.4 | async-start | bytes 1671168 | tf_op jit(solution)/shard_map/all_to_all | solution.py:822
  313.0 2.2 convert_add_fusion.1
  317.1 2.8 fusion.9
  319.9 1.4 add_multiply_fusion.2
  321.8 2.5 fusion.4
  324.4 8.9 %all-to-all-done.4.found_ref = bf16[4,48,2064]{2,1,0:T(8,128)(2,1)S(1)} async-done(((bf16[4,48,2064]{2,1,0:T(8,128)(2,1)}), bf16[4,48,2064]{2,1,0:T(8,128)(2,1)S(1)}, u32[]{:S(2)}, u32[]{:S(2)}) %all-to-all-start.4) | async-done | bytes 792608 | tf_op jit(solution)/shard_map/all_to_all | solution.py:822
  333.9 1.3 copy-done.5
  335.3 3.3 finish_weight.1
  (254 shorter events, 28.0 us)
Async XLA Ops:
  0.7 5.7 %slice-start = ((bf16[384,6448]{0,1:T(8,128)(2,1)}), bf16[384,48]{0,1:T(8,128)(2,1)S(1)}, s32[]{:S(2)}) async-start(bf16[384,6448]{0,1:T(8,128)(2,1)} %param.25), calls=%async_computation.5 | async-start | bytes 73728 | tf_op jit(solution)/shard_map/slice | solution.py:884
  0.7 5.8 %copy-start.39 = (bf16[5,832]{1,0:T(8,128)(2,1)S(1)}, bf16[5,832]{1,0:T(8,128)(2,1)}, u32[]{:S(2)}) copy-start(bf16[5,832]{1,0:T(8,128)(2,1)} %param.28) | copy-start | bytes 24964
  0.7 5.9 %copy-start.48 = (bf16[3,12]{1,0:T(4,128)(2,1)S(1)}, bf16[3,12]{1,0:T(4,128)(2,1)}, u32[]{:S(2)}) copy-start(bf16[3,12]{1,0:T(4,128)(2,1)} %param.31) | copy-start | bytes 220
  0.7 5.9 %copy-start.44 = (bf16[384]{0:T(512)(128)(2,1)S(1)}, bf16[384]{0:T(512)(128)(2,1)}, u32[]{:S(2)}) copy-start(bf16[384]{0:T(512)(128)(2,1)} %param.22) | copy-start | bytes 2308
  0.7 5.9 %copy-start.43 = (bf16[768]{0:T(1024)(128)(2,1)S(1)}, bf16[768]{0:T(1024)(128)(2,1)}, u32[]{:S(2)}) copy-start(bf16[768]{0:T(1024)(128)(2,1)} %param.34) | copy-start | bytes 4612
  1.9 5.9 %collective-permute-start = (bf16[128,1536]{1,0:T(8,128)(2,1)S(1)}, bf16[128,1536]{1,0:T(8,128)(2,1)S(1)}, u32[]{:S(2)}, u32[]{:S(2)}) collective-permute-start(bf16[128,1536]{1,0:T(8,128)(2,1)S(1)} %get-tuple-element.288), channel_id=1, source_target_pairs={{0,1},{1,0},{2,3},{3,2},{4,5},{5,4},{6,7},{7,6},{8,9},{9,8},{10,11... | collective-permute-start | bytes 1179656 | tf_op jit(solution)/shard_map/ppermute | solution.py:803
  8.0 10.5 %copy-start.6 = (bf16[256,1536]{1,0:T(8,128)(2,1)}, bf16[256,1536]{1,0:T(8,128)(2,1)S(1)}, u32[]{:S(2)}) copy-start(bf16[256,1536]{1,0:T(8,128)(2,1)S(1)} %maximum_select_fusion.3.refs_0_) | copy-start | bytes 2359300
  9.8 4.9 %copy-start.19 = (bf16[2,128,1536]{2,1,0:T(8,128)(2,1)S(1)}, bf16[2,128,1536]{2,1,0:T(8,128)(2,1)}, u32[]{:S(2)}) copy-start(bf16[2,128,1536]{2,1,0:T(8,128)(2,1)} %param.21) | copy-start | bytes 2359300
  9.8 45.7 %all-to-all-start = ((bf16[4,928,384]{2,1,0:T(8,128)(2,1)}), bf16[4,928,384]{2,1,0:T(8,128)(2,1)}, u32[]{:S(2)}, u32[]{:S(2)}) async-start(bf16[4,928,384]{2,1,0:T(8,128)(2,1)} %broadcast_in_dim.18), calls=%async_computation | async-start | bytes 5701632 | tf_op jit(solution)/shard_map/all_to_all | solution.py:815
  15.5 11.3 %collective-permute-start.1 = (bf16[128,1536]{1,0:T(8,128)(2,1)}, bf16[128,1536]{1,0:T(8,128)(2,1)}, u32[]{:S(2)}, u32[]{:S(2)}) collective-permute-start(bf16[128,1536]{1,0:T(8,128)(2,1)} %get-tuple-element.286), channel_id=1, source_target_pairs={{0,1},{1,0},{2,3},{3,2},{4,5},{5,4},{6,7},{7,6},{8,9},{9,8},{10,11... | collective-permute-start | bytes 1179656 | tf_op jit(solution)/shard_map/ppermute | solution.py:803
  15.7 37.3 %collective-permute-start.2 = (bf16[256,1536]{1,0:T(8,128)(2,1)S(1)}, bf16[256,1536]{1,0:T(8,128)(2,1)S(1)}, u32[]{:S(2)}, u32[]{:S(2)}) collective-permute-start(bf16[256,1536]{1,0:T(8,128)(2,1)S(1)} %maximum_select_fusion.3.refs_0_), channel_id=1, source_target_pairs={{0,2},{1,3},{2,0},{3,1},{4,6},{5,7},{6,4},{7,5},{8,10},{9,11},{10,... | collective-permute-start | bytes 2359304 | tf_op jit(solution)/shard_map/ppermute | solution.py:809
  18.4 37.0 %collective-permute-start.3 = (bf16[256,1536]{1,0:T(8,128)(2,1)S(1)}, bf16[256,1536]{1,0:T(8,128)(2,1)S(1)}, u32[]{:S(2)}, u32[]{:S(2)}) collective-permute-start(bf16[256,1536]{1,0:T(8,128)(2,1)S(1)} %maximum_select_fusion.3.refs_0_), channel_id=1, source_target_pairs={{0,4},{1,5},{2,6},{3,7},{4,0},{5,1},{6,2},{7,3},{8,12},{9,13},{10,... | collective-permute-start | bytes 2359304 | tf_op jit(solution)/shard_map/ppermute | solution.py:809
  26.7 137.2 %copy-start.9 = (s32[5]{0:T(128)}, s32[5]{0:T(128)S(1)}, u32[]{:S(2)}) copy-start(s32[5]{0:T(128)S(1)} %pad_add_fusion.order_ref) | copy-start | bytes 64
  52.9 9.7 %copy-start.12 = (bf16[256,1536]{1,0:T(8,128)(2,1)}, bf16[256,1536]{1,0:T(8,128)(2,1)S(1)}, u32[]{:S(2)}) copy-start(bf16[256,1536]{1,0:T(8,128)(2,1)S(1)} %collective-permute-done.2.refs_1_) | copy-start | bytes 2359300
  55.5 7.2 %copy-start.14 = (bf16[256,1536]{1,0:T(8,128)(2,1)}, bf16[256,1536]{1,0:T(8,128)(2,1)S(1)}, u32[]{:S(2)}) copy-start(bf16[256,1536]{1,0:T(8,128)(2,1)S(1)} %collective-permute-done.3.refs_2_) | copy-start | bytes 2359300
  56.3 57.8 %collective-permute-start.8 = (bf16[4,928,384]{2,1,0:T(8,128)(2,1)}, bf16[4,928,384]{2,1,0:T(8,128)(2,1)}, u32[]{:S(2)}, u32[]{:S(2)}) collective-permute-start(bf16[4,928,384]{2,1,0:T(8,128)(2,1)} %all-to-all-done.refs_7_), channel_id=1, source_target_pairs={{0,1},{1,0},{2,3},{3,2},{4,5},{5,4},{6,7},{7,6},{8,9},{9,8},{10,11... | collective-permute-start | bytes 8552456 | tf_op jit(solution)/shard_map/ppermute | solution.py:803
  56.3 10.9 %copy-start.36 = (bf16[1,4,16,384]{3,1,2,0:T(4,128)(2,1)}, bf16[1,4,16,384]{3,1,2,0:T(4,128)(2,1)S(1)}, u32[]{:S(2)}) copy-start(bf16[1,4,16,384]{3,1,2,0:T(4,128)(2,1)S(1)} %copy.94) | copy-start | bytes 147460
  56.6 54.0 %collective-permute-start.6 = (bf16[256,1536]{1,0:T(8,128)(2,1)}, bf16[256,1536]{1,0:T(8,128)(2,1)}, u32[]{:S(2)}, u32[]{:S(2)}) collective-permute-start(bf16[256,1536]{1,0:T(8,128)(2,1)} %maximum_select_fusion.4.refs_0_), channel_id=1, source_target_pairs={{0,2},{1,3},{2,0},{3,1},{4,6},{5,7},{6,4},{7,5},{8,10},{9,11},{10,... | collective-permute-start | bytes 2359304 | tf_op jit(solution)/shard_map/ppermute | solution.py:809
  57.1 53.5 %collective-permute-start.7 = (bf16[256,1536]{1,0:T(8,128)(2,1)}, bf16[256,1536]{1,0:T(8,128)(2,1)}, u32[]{:S(2)}, u32[]{:S(2)}) collective-permute-start(bf16[256,1536]{1,0:T(8,128)(2,1)} %maximum_select_fusion.4.refs_0_), channel_id=1, source_target_pairs={{0,4},{1,5},{2,6},{3,7},{4,0},{5,1},{6,2},{7,3},{8,12},{9,13},{10,... | collective-permute-start | bytes 2359304 | tf_op jit(solution)/shard_map/ppermute | solution.py:809
  62.7 31.9 %all-to-all-start.1 = ((bf16[4,192,1536]{2,1,0:T(8,128)(2,1)}), bf16[4,192,1536]{2,1,0:T(8,128)(2,1)S(1)}, u32[]{:S(2)}, u32[]{:S(2)}) async-start(bf16[4,192,1536]{2,1,0:T(8,128)(2,1)} %broadcast_in_dim.19), calls=%async_computation.1 | async-start | bytes 4718592 | tf_op jit(solution)/shard_map/all_to_all | solution.py:815
  67.1 47.0 %copy-start.8 = (f32[16,128]{1,0:T(8,128)}, f32[16,128]{1,0:T(8,128)S(1)}, u32[]{:S(2)}) copy-start(f32[16,128]{1,0:T(8,128)S(1)} %pad.31.refs_6_.head_ref) | copy-start | bytes 24580
  67.4 35.9 %collective-permute-start.4 = (bf16[256,1536]{1,0:T(8,128)(2,1)}, bf16[256,1536]{1,0:T(8,128)(2,1)}, u32[]{:S(2)}, u32[]{:S(2)}) collective-permute-start(bf16[256,1536]{1,0:T(8,128)(2,1)} %copy-done.6), channel_id=1, source_target_pairs={{2,4},{3,5},{4,2},{5,3},{10,12},{11,13},{12,10},{13,11},{18,20},{1... | collective-permute-start | bytes 2359304 | tf_op jit(solution)/shard_map/ppermute | solution.py:809
  69.0 41.7 %collective-permute-start.5 = (bf16[256,1536]{1,0:T(8,128)(2,1)}, bf16[256,1536]{1,0:T(8,128)(2,1)}, u32[]{:S(2)}, u32[]{:S(2)}) collective-permute-start(bf16[256,1536]{1,0:T(8,128)(2,1)} %copy-done.14), channel_id=1, source_target_pairs={{2,0},{3,1},{4,6},{5,7},{10,8},{11,9},{12,14},{13,15},{18,16},{19,... | collective-permute-start | bytes 2359304 | tf_op jit(solution)/shard_map/ppermute | solution.py:809
  72.1 91.9 %copy-start.2 = (f32[8,1024]{0,1:T(8,128)}, f32[8,1024]{0,1:T(8,128)S(1)}, u32[]{:S(2)}) copy-start(f32[8,1024]{0,1:T(8,128)S(1)} %copy.85) | copy-start | bytes 98308
  98.3 72.5 %all-to-all-start.2 = ((bf16[4,768,768]{2,1,0:T(8,128)(2,1)}), bf16[4,768,768]{2,1,0:T(8,128)(2,1)}, u32[]{:S(2)}, u32[]{:S(2)}) async-start(bf16[4,768,768]{2,1,0:T(8,128)(2,1)} %broadcast_in_dim.22), calls=%async_computation.2 | async-start | bytes 9437184 | tf_op jit(solution)/shard_map/all_to_all | solution.py:815
  103.3 10.9 %copy-start.7 = (bf16[256,1536]{1,0:T(8,128)(2,1)S(1)}, bf16[256,1536]{1,0:T(8,128)(2,1)}, u32[]{:S(2)}) copy-start(bf16[256,1536]{1,0:T(8,128)(2,1)} %copy-done.6) | copy-start | bytes 2359300
  103.3 10.9 %copy-start.13 = (bf16[256,1536]{1,0:T(8,128)(2,1)S(1)}, bf16[256,1536]{1,0:T(8,128)(2,1)}, u32[]{:S(2)}) copy-start(bf16[256,1536]{1,0:T(8,128)(2,1)} %copy-done.12) | copy-start | bytes 2359300
  103.3 10.8 %copy-start.15 = (bf16[256,1536]{1,0:T(8,128)(2,1)S(1)}, bf16[256,1536]{1,0:T(8,128)(2,1)}, u32[]{:S(2)}) copy-start(bf16[256,1536]{1,0:T(8,128)(2,1)} %copy-done.14) | copy-start | bytes 2359300
  110.7 30.9 %collective-permute-start.10 = (bf16[256,1536]{1,0:T(8,128)(2,1)}, bf16[256,1536]{1,0:T(8,128)(2,1)S(1)}, u32[]{:S(2)}, u32[]{:S(2)}) collective-permute-start(bf16[256,1536]{1,0:T(8,128)(2,1)} %collective-permute-done.7.refs_2_), channel_id=1, source_target_pairs={{2,0},{3,1},{4,6},{5,7},{10,8},{11,9},{12,14},{13,15},{18,16},{19,... | collective-permute-start | bytes 2359304 | tf_op jit(solution)/shard_map/ppermute | solution.py:809
  112.0 29.6 %collective-permute-start.9 = (bf16[256,1536]{1,0:T(8,128)(2,1)}, bf16[256,1536]{1,0:T(8,128)(2,1)S(1)}, u32[]{:S(2)}, u32[]{:S(2)}) collective-permute-start(bf16[256,1536]{1,0:T(8,128)(2,1)} %maximum_select_fusion.4.refs_0_), channel_id=1, source_target_pairs={{2,4},{3,5},{4,2},{5,3},{10,12},{11,13},{12,10},{13,11},{18,20},{1... | collective-permute-start | bytes 2359304 | tf_op jit(solution)/shard_map/ppermute | solution.py:809
  144.1 19.8 %copy-start.1 = (f32[768,1024]{1,0:T(8,128)S(1)}, f32[768,1024]{1,0:T(8,128)}, u32[]{:S(2)}) copy-start(f32[768,1024]{1,0:T(8,128)} %get-tuple-element.158.gates_ref) | copy-start | bytes 9437188
  153.0 7.8 %collective-permute-start.11 = (f32[2,1024]{1,0:T(2,128)S(1)}, f32[2,1024]{1,0:T(2,128)S(1)}, u32[]{:S(2)}, u32[]{:S(2)}) collective-permute-start(f32[2,1024]{1,0:T(2,128)S(1)} %slice.123), channel_id=1, source_target_pairs={{0,2},{1,3},{2,0},{3,1},{4,6},{5,7},{6,4},{7,5},{8,10},{9,11},{10,... | collective-permute-start | bytes 24584 | tf_op jit(solution)/shard_map/ppermute | solution.py:809
  158.4 4.5 %collective-permute-start.12 = (f32[2,1024]{1,0:T(2,128)S(1)}, f32[2,1024]{1,0:T(2,128)S(1)}, u32[]{:S(2)}, u32[]{:S(2)}) collective-permute-start(f32[2,1024]{1,0:T(2,128)S(1)} %slice.123), channel_id=1, source_target_pairs={{0,4},{1,5},{2,6},{3,7},{4,0},{5,1},{6,2},{7,3},{8,12},{9,13},{10,... | collective-permute-start | bytes 24584 | tf_op jit(solution)/shard_map/ppermute | solution.py:809
  158.4 5.4 %collective-permute-start.13 = (f32[2,1024]{1,0:T(2,128)S(1)}, f32[2,1024]{1,0:T(2,128)S(1)}, u32[]{:S(2)}, u32[]{:S(2)}) collective-permute-start(f32[2,1024]{1,0:T(2,128)S(1)} %slice.123), channel_id=1, source_target_pairs={{0,6},{1,7},{2,4},{3,5},{4,2},{5,3},{6,0},{7,1},{8,14},{9,15},{10,... | collective-permute-start | bytes 24584 | tf_op jit(solution)/shard_map/ppermute | solution.py:809
  183.3 39.3 %collective-permute-start.18 = (bf16[4,4,48,768]{3,2,1,0:T(8,128)(2,1)}, bf16[4,4,48,768]{3,2,1,0:T(8,128)(2,1)S(1)}, u32[]{:S(2)}, u32[]{:S(2)}) collective-permute-start(bf16[4,4,48,768]{3,2,1,0:T(8,128)(2,1)} %bitcast.115), channel_id=1, source_target_pairs={{0,1},{1,0},{2,3},{3,2},{4,5},{5,4},{6,7},{7,6},{8,9},{9,8},{10,11... | collective-permute-start | bytes 3538952 | tf_op jit(solution)/shard_map/ppermute | solution.py:803
  183.3 39.3 %collective-permute-start.17 = (bf16[4,96,1536]{2,1,0:T(8,128)(2,1)S(1)}, bf16[4,96,1536]{2,1,0:T(8,128)(2,1)S(1)}, u32[]{:S(2)}, u32[]{:S(2)}) collective-permute-start(bf16[4,96,1536]{2,1,0:T(8,128)(2,1)S(1)} %get-tuple-element.268), channel_id=1, source_target_pairs={{0,1},{1,0},{2,3},{3,2},{4,5},{5,4},{6,7},{7,6},{8,9},{9,8},{10,11... | collective-permute-start | bytes 3538952 | tf_op jit(solution)/shard_map/ppermute | solution.py:803
  183.8 38.7 %collective-permute-start.14 = (bf16[768,256]{1,0:T(8,128)(2,1)}, bf16[768,256]{1,0:T(8,128)(2,1)S(1)}, u32[]{:S(2)}, u32[]{:S(2)}) collective-permute-start(bf16[768,256]{1,0:T(8,128)(2,1)} %get-tuple-element.280), channel_id=1, source_target_pairs={{0,2},{1,3},{2,0},{3,1},{4,6},{5,7},{6,4},{7,5},{8,10},{9,11},{10,... | collective-permute-start | bytes 1179656 | tf_op jit(solution)/shard_map/ppermute | solution.py:809
  183.9 38.6 %collective-permute-start.15 = (bf16[768,256]{1,0:T(8,128)(2,1)}, bf16[768,256]{1,0:T(8,128)(2,1)S(1)}, u32[]{:S(2)}, u32[]{:S(2)}) collective-permute-start(bf16[768,256]{1,0:T(8,128)(2,1)} %get-tuple-element.279), channel_id=1, source_target_pairs={{0,4},{1,5},{2,6},{3,7},{4,0},{5,1},{6,2},{7,3},{8,12},{9,13},{10,... | collective-permute-start | bytes 1179656 | tf_op jit(solution)/shard_map/ppermute | solution.py:809
  186.7 35.8 %collective-permute-start.16 = (bf16[768,256]{1,0:T(8,128)(2,1)}, bf16[768,256]{1,0:T(8,128)(2,1)S(1)}, u32[]{:S(2)}, u32[]{:S(2)}) collective-permute-start(bf16[768,256]{1,0:T(8,128)(2,1)} %get-tuple-element.278), channel_id=1, source_target_pairs={{0,6},{1,7},{2,4},{3,5},{4,2},{5,3},{6,0},{7,1},{8,14},{9,15},{10,... | collective-permute-start | bytes 1179656 | tf_op jit(solution)/shard_map/ppermute | solution.py:809
  222.6 18.1 %collective-permute-start.21 = (bf16[3072,768]{1,0:T(8,128)(2,1)}, bf16[3072,768]{1,0:T(8,128)(2,1)}, u32[]{:S(2)}, u32[]{:S(2)}) collective-permute-start(bf16[3072,768]{1,0:T(8,128)(2,1)} %bitcast.22), channel_id=1, source_target_pairs={{0,1},{1,0},{2,3},{3,2},{4,5},{5,4},{6,7},{7,6},{8,9},{9,8},{10,11... | collective-permute-start | bytes 14155784 | tf_op jit(solution)/shard_map/ppermute | solution.py:803
  223.7 17.0 %collective-permute-start.20 = (bf16[4,4,48,1040]{3,2,1,0:T(8,128)(2,1)}, bf16[4,4,48,1040]{3,2,1,0:T(8,128)(2,1)}, u32[]{:S(2)}, u32[]{:S(2)}) collective-permute-start(bf16[4,4,48,1040]{3,2,1,0:T(8,128)(2,1)} %bitcast.114), channel_id=1, source_target_pairs={{0,1},{1,0},{2,3},{3,2},{4,5},{5,4},{6,7},{7,6},{8,9},{9,8},{10,11... | collective-permute-start | bytes 4792328 | tf_op jit(solution)/shard_map/ppermute | solution.py:803
  227.8 12.9 %collective-permute-start.19 = (f32[5156]{0:T(1024)S(1)}, f32[5156]{0:T(1024)S(1)}, u32[]{:S(2)}, u32[]{:S(2)}) collective-permute-start(f32[5156]{0:T(1024)S(1)} %constant_dynamic-update-slice_fusion.2), channel_id=1, source_target_pairs={{0,1},{1,0},{2,3},{3,2},{4,5},{5,4},{6,7},{7,6},{8,9},{9,8},{10,11... | collective-permute-start | bytes 61880 | tf_op jit(solution)/shard_map/ppermute | solution.py:803
  228.4 16.2 %copy-start.23 = (bf16[16,48,1040]{2,1,0:T(8,128)(2,1)S(1)}, bf16[16,48,1040]{2,1,0:T(8,128)(2,1)}, u32[]{:S(2)}) copy-start(bf16[16,48,1040]{2,1,0:T(8,128)(2,1)} %get-tuple-element.183) | copy-start | bytes 4792324
  240.7 18.9 %collective-permute-start.22 = (bf16[256,1536]{1,0:T(8,128)(2,1)}, bf16[256,1536]{1,0:T(8,128)(2,1)}, u32[]{:S(2)}, u32[]{:S(2)}) collective-permute-start(bf16[256,1536]{1,0:T(8,128)(2,1)} %get-tuple-element.206), channel_id=1, source_target_pairs={{0,2},{1,3},{6,4},{7,5},{8,10},{9,11},{14,12},{15,13},{16,18},{17,... | collective-permute-start | bytes 2359304 | tf_op jit(solution)/shard_map/ppermute | solution.py:809
  243.0 16.7 %collective-permute-start.23 = (bf16[256,1536]{1,0:T(8,128)(2,1)}, bf16[256,1536]{1,0:T(8,128)(2,1)}, u32[]{:S(2)}, u32[]{:S(2)}) collective-permute-start(bf16[256,1536]{1,0:T(8,128)(2,1)} %get-tuple-element.206), channel_id=1, source_target_pairs={{2,4},{3,5},{4,2},{5,3},{10,12},{11,13},{12,10},{13,11},{18,20},{1... | collective-permute-start | bytes 2359304 | tf_op jit(solution)/shard_map/ppermute | solution.py:809
  248.9 55.4 %all-to-all-start.3 = ((bf16[4,192,2704]{2,1,0:T(8,128)(2,1)}), bf16[4,192,2704]{2,1,0:T(8,128)(2,1)}, u32[]{:S(2)}, u32[]{:S(2)}) async-start(bf16[4,192,2704]{2,1,0:T(8,128)(2,1)} %pad_maximum_fusion), calls=%async_computation.3 | async-start | bytes 8650752 | tf_op jit(solution)/shard_map/all_to_all | solution.py:815
  259.6 35.6 %collective-permute-start.24 = (bf16[256,1536]{1,0:T(8,128)(2,1)}, bf16[256,1536]{1,0:T(8,128)(2,1)S(1)}, u32[]{:S(2)}, u32[]{:S(2)}) collective-permute-start(bf16[256,1536]{1,0:T(8,128)(2,1)} %get-tuple-element.207), channel_id=1, source_target_pairs={{0,2},{1,3},{2,0},{3,1},{4,6},{5,7},{6,4},{7,5},{8,10},{9,11},{10,... | collective-permute-start | bytes 2359304 | tf_op jit(solution)/shard_map/ppermute | solution.py:809
  263.0 32.3 %copy-start.31 = (bf16[768,256]{1,0:T(8,128)(2,1)S(1)}, bf16[768,256]{1,0:T(8,128)(2,1)}, u32[]{:S(2)}) copy-start(bf16[768,256]{1,0:T(8,128)(2,1)} %copy-done.30) | copy-start | bytes 1179652
  263.0 32.3 %copy-start.33 = (bf16[768,256]{1,0:T(8,128)(2,1)S(1)}, bf16[768,256]{1,0:T(8,128)(2,1)}, u32[]{:S(2)}) copy-start(bf16[768,256]{1,0:T(8,128)(2,1)} %copy-done.32) | copy-start | bytes 1179652
  263.0 32.3 %copy-start.35 = (bf16[768,256]{1,0:T(8,128)(2,1)S(1)}, bf16[768,256]{1,0:T(8,128)(2,1)}, u32[]{:S(2)}) copy-start(bf16[768,256]{1,0:T(8,128)(2,1)} %copy-done.34) | copy-start | bytes 1179652
  264.7 39.6 %collective-permute-start.25 = (bf16[256,1536]{1,0:T(8,128)(2,1)S(1)}, bf16[256,1536]{1,0:T(8,128)(2,1)}, u32[]{:S(2)}, u32[]{:S(2)}) collective-permute-start(bf16[256,1536]{1,0:T(8,128)(2,1)S(1)} %add_convert_fusion.3), channel_id=1, source_target_pairs={{0,4},{1,5},{2,6},{3,7},{4,0},{5,1},{6,2},{7,3},{8,12},{9,13},{10,... | collective-permute-start | bytes 2359304 | tf_op jit(solution)/shard_map/ppermute | solution.py:809
  309.5 23.7 %all-to-all-start.4 = ((bf16[4,48,2064]{2,1,0:T(8,128)(2,1)}), bf16[4,48,2064]{2,1,0:T(8,128)(2,1)S(1)}, u32[]{:S(2)}, u32[]{:S(2)}) async-start(bf16[4,48,2064]{2,1,0:T(8,128)(2,1)} %pad_maximum_fusion.4), calls=%async_computation.4 | async-start | bytes 1671168 | tf_op jit(solution)/shard_map/all_to_all | solution.py:822
  315.3 6.0 %collective-permute-start.27 = (f32[1,128,1536]{2,1,0:T(8,128)S(1)}, f32[1,128,1536]{2,1,0:T(8,128)S(1)}, u32[]{:S(2)}, u32[]{:S(2)}) collective-permute-start(f32[1,128,1536]{2,1,0:T(8,128)S(1)} %get-tuple-element.270), channel_id=1, source_target_pairs={{0,1},{1,0},{2,3},{3,2},{4,5},{5,4},{6,7},{7,6},{8,9},{9,8},{10,11... | collective-permute-start | bytes 2359304 | tf_op jit(solution)/shard_map/ppermute | solution.py:803
  315.6 6.2 %collective-permute-start.26 = (f32[1,128,1536]{2,1,0:T(8,128)S(1)}, f32[1,128,1536]{2,1,0:T(8,128)S(1)}, u32[]{:S(2)}, u32[]{:S(2)}) collective-permute-start(f32[1,128,1536]{2,1,0:T(8,128)S(1)} %get-tuple-element.273), channel_id=1, source_target_pairs={{0,1},{1,0},{2,3},{3,2},{4,5},{5,4},{6,7},{7,6},{8,9},{9,8},{10,11... | collective-permute-start | bytes 2359304 | tf_op jit(solution)/shard_map/ppermute | solution.py:803
  317.0 4.3 %copy-start.17 = (bf16[2,128,1536]{2,1,0:T(8,128)(2,1)S(1)}, bf16[2,128,1536]{2,1,0:T(8,128)(2,1)}, u32[]{:S(2)}) copy-start(bf16[2,128,1536]{2,1,0:T(8,128)(2,1)} %param.20) | copy-start | bytes 2359300
  324.4 9.6 %copy-start.4 = (f32[48,6448]{1,0:T(8,128)S(1)}, f32[48,6448]{1,0:T(8,128)}, u32[]{:S(2)}) copy-start(f32[48,6448]{1,0:T(8,128)} %first_ref.1) | copy-start | bytes 3714052
  335.2 3.7 %copy-start.45 = (bf16[384]{0:T(512)(128)(2,1)S(1)}, bf16[384]{0:T(512)(128)(2,1)}, u32[]{:S(2)}) copy-start(bf16[384]{0:T(512)(128)(2,1)} %param.22) | copy-start | bytes 2308
  335.2 3.7 %copy-start.52 = (f32[48]{0:T(128)S(1)}, f32[48]{0:T(128)}, u32[]{:S(2)}) copy-start(f32[48]{0:T(128)} %param.24) | copy-start | bytes 580
  335.2 3.7 %copy-start.53 = (f32[48]{0:T(128)S(1)}, f32[48]{0:T(128)}, u32[]{:S(2)}) copy-start(f32[48]{0:T(128)} %param.23) | copy-start | bytes 580
  335.2 4.3 %copy-start.46 = (f32[3,12]{1,0:T(4,128)S(1)}, f32[3,12]{1,0:T(4,128)}, u32[]{:S(2)}) copy-start(f32[3,12]{1,0:T(4,128)} %param.33) | copy-start | bytes 436
  335.2 4.3 %copy-start.47 = (f32[3,12]{1,0:T(4,128)S(1)}, f32[3,12]{1,0:T(4,128)}, u32[]{:S(2)}) copy-start(f32[3,12]{1,0:T(4,128)} %param.32) | copy-start | bytes 436
  335.2 4.3 %copy-start.49 = (bf16[3,12]{1,0:T(4,128)(2,1)S(1)}, bf16[3,12]{1,0:T(4,128)(2,1)}, u32[]{:S(2)}) copy-start(bf16[3,12]{1,0:T(4,128)(2,1)} %param.31) | copy-start | bytes 220
  335.3 5.0 %copy-start.41 = (f32[5,104]{1,0:T(8,128)S(1)}, f32[5,104]{1,0:T(8,128)}, u32[]{:S(2)}) copy-start(f32[5,104]{1,0:T(8,128)} %param.30) | copy-start | bytes 6244
  335.3 5.0 %copy-start.42 = (f32[5,104]{1,0:T(8,128)S(1)}, f32[5,104]{1,0:T(8,128)}, u32[]{:S(2)}) copy-start(f32[5,104]{1,0:T(8,128)} %param.29) | copy-start | bytes 6244
  (24 other events, 40.8 us)
where the time goes:
time: 347 us; the launch traced here: 341 us
  waiting for transfers between devices  100 us (29%)
  Pallas kernels  95.5 us (28%)
  starting transfers between devices  58.9 us (17%)
  local copies, waits for them, and re-layouts  41.5 us (12%)
  other arithmetic  30.4 us (9%)
  matrix products  12.2 us (4%)
    ppermute x18, waiting for transfers between devices, along(): return lax.ppermute(x, 'seq', pairs)  72.1 us
    ppermute x18, starting transfers between devices, along(): return lax.ppermute(x, 'seq', pairs)  33.8 us
    pallas_call x1, Pallas kernels, run_forward(): pl.pallas_call(functools.partial(mixer_forward, own_width, heads, kernel_...  27.4 us
    pallas_call x1, Pallas kernels, run_backward(): pl.pallas_call(functools.partial(mixer_backward, own_width, heads, kernel...  26 us
    all_to_all x4, waiting for transfers between devices, shard_exchange(): return lax.all_to_all(x, 'wshard', split_axis=0, concat_axis=0, tiled=True)  19.4 us
    all_to_all x4, starting transfers between devices, shard_exchange(): return lax.all_to_all(x, 'wshard', split_axis=0, concat_axis=0, tiled=True)  19.1 us
    unnamed x119, local copies, waits for them, and re-layouts  17 us
    pallas_call x2, Pallas kernels, run_weight_gradient(): pl.pallas_call(functools.partial(weight_gradient, in_rows), grid_spec=spe...  14.9 us
  transfers between devices with their start and end apart: 33, of which 9 were waited for; matrix products, arithmetic and copies ran while one was open for 16% of the time, Pallas kernels for 25%

commit v1 on v0

--- a/solution.py
+++ b/solution.py
@@ -86,7 +86,7 @@
 def mixer_forward(own_width, heads, kernel_len, places, start, assemble, order_ref, *refs):
     token_refs = refs[:places]
     gain_ref, chan_ref, head_ref = refs[places : places + 3]
-    given = refs[places + 3 : -14]
+    given = refs[places + 3 : -15]
     (
         weight_out,
         normed_ref,
@@ -102,7 +102,8 @@
         steps,
         inter,
         scaled,
-    ) = refs[-14:]
+        wide,
+    ) = refs[-15:]
     channels = chan_ref.shape[0]
     width = own_width // heads
     token_block = normed_ref.shape[0]
@@ -111,6 +112,8 @@
     def _():
         before[...] = given[1][...] if start else jnp.zeros_like(before)
         state[...] = given[2][...] if start else jnp.zeros_like(state)
+        for at, column in enumerate((*range(kernel_len + 1), 6)):
+            wide[at] = jnp.broadcast_to(chan_ref[:, column : column + 1], wide.shape[1:])
         if not assemble:
             weight_out[...] = jnp.zeros_like(weight_out)
         else:
@@ -141,11 +144,10 @@
             raw = values_ref[rows, here]
             current = raw.astype(f32)
             previous = before[rows, :].astype(f32)
-            taps = chan_ref[rows, :]
-            out = taps[:, kernel_len : kernel_len + 1] + taps[:, kernel_len - 1 : kernel_len] * current
+            out = wide[kernel_len, rows, :] + wide[kernel_len - 1, rows, :] * current
             for shift in range(1, kernel_len):
                 tap = kernel_len - 1 - shift
-                out = out + taps[:, tap : tap + 1] * earlier_by(current, previous, lane, shift)
+                out = out + wide[tap, rows, :] * earlier_by(current, previous, lane, shift)
             before[rows, :] = raw
             conv_ref[rows, here] = out
             active[rows, :] = out * sigmoid(out)
@@ -179,7 +181,7 @@
             driven = (x * step[head : head + 1, :]).astype(bf16)
             mixed = dot_nn(driven, weights)
             mixed = mixed + inter[rows, :] * grow[head : head + 1, :]
-            mixed = mixed + chan_ref[rows, 6:7] * x
+            mixed = mixed + wide[kernel_len + 1, rows, :] * x
             sent_ref[rows, here] = mixed.astype(bf16)
             scaled[rows, :] = (x * tail[head : head + 1, :]).astype(bf16)
             state[rows, :] = state[rows, :] * total_decay[head : head + 1, :]
@@ -258,6 +260,7 @@
         driven,
         tailed,
         rows_scr,
+        wide,
     ) = refs
     channels = chan_ref.shape[0]
     width = own_width // heads
@@ -268,6 +271,8 @@
         for held in (conv_acc, head_acc, adjoint, following):
             held[...] = jnp.zeros_like(held)
         rows_scr[...] = jnp.zeros_like(rows_scr)
+        for at, column in enumerate((*range(kernel_len), 6)):
+            wide[at] = jnp.broadcast_to(chan_ref[:, column : column + 1], wide.shape[1:])
 
     lane = lanes((Q, Q))
     sub = lax.broadcasted_iota(jnp.int32, (Q, Q), 0)
@@ -333,7 +338,7 @@
                 rows_scr[4, one, :] = jnp.sum(grad * x, axis=0, keepdims=True)
                 old = adjoint[rows, :]
                 rows_scr[5, one, :] = jnp.sum(old * held[rows, :].astype(f32), axis=0, keepdims=True)
-                dactive[rows, :] = back * step[one, :] + chan_ref[rows, 6:7] * grad
+                dactive[rows, :] = back * step[one, :] + wide[kernel_len, rows, :] * grad
                 driven[rows, :] = (grad * grow[one, :]).astype(bf16)
                 tailed[rows, :] = (x * tail[one, :]).astype(bf16)
                 adjoint[rows, :] = old * total_decay[one, :]
@@ -359,15 +364,14 @@
             conv = conv_ref[rows, here]
             sig = sigmoid(conv)
             dconv = dactive[rows, :] * sig * (1.0 + conv * (1.0 - sig))
-            taps = chan_ref[rows, :]
             raw = values_ref[rows, here].astype(f32)
             nxt = following[rows, :]
-            dvalue = taps[:, kernel_len - 1 : kernel_len] * dconv
+            dvalue = wide[kernel_len - 1, rows, :] * dconv
             conv_acc[kernel_len - 1, rows, :] += raw * dconv
             for shift in range(1, kernel_len):
                 tap = kernel_len - 1 - shift
                 moved = later_by(dconv, nxt, lane, shift)
-                dvalue = dvalue + taps[:, tap : tap + 1] * moved
+                dvalue = dvalue + wide[tap, rows, :] * moved
                 conv_acc[tap, rows, :] += raw * moved
             conv_acc[kernel_len, rows, :] += dconv
             following[rows, :] = dconv
@@ -428,6 +432,7 @@
             pltpu.VMEM((HP, token_block), f32),
             pltpu.VMEM((own_width, Q), f32),
             pltpu.VMEM((own_width, Q), bf16),
+            pltpu.VMEM((kernel_len + 2, channels, Q), f32),
         ],
     )
     found = pl.pallas_call(
@@ -574,6 +579,7 @@
             pltpu.VMEM((own_width, Q), bf16),
             pltpu.VMEM((own_width, Q), bf16),
             pltpu.VMEM((6, HP, Q), f32),
+            pltpu.VMEM((kernel_len + 1, channels, Q), f32),
         ],
     )
     return pl.pallas_call(

time: 347 us -> 346 us (level)
  Pallas kernels: 95.5 us -> 92 us
  transfers between devices with their start and end apart: 33 -> 33, of which waited for: 9 -> 9; matrix products, arithmetic and copies ran while one was open for 16% -> 16% of each run, Pallas kernels for 25% -> 24%
where the time goes in v1:
time: 346 us; the launch traced here: 340 us
  waiting for transfers between devices  100 us (29%)
  Pallas kernels  92 us (27%)
  starting transfers between devices  61.1 us (18%)
  local copies, waits for them, and re-layouts  41.5 us (12%)
  other arithmetic  30.4 us (9%)
  matrix products  12.2 us (4%)
    ppermute x18, waiting for transfers between devices, along(): return lax.ppermute(x, 'seq', pairs)  71.9 us
    ppermute x18, starting transfers between devices, along(): return lax.ppermute(x, 'seq', pairs)  36 us
    pallas_call x1, Pallas kernels, run_forward(): pl.pallas_call(functools.partial(mixer_forward, own_width, heads, kernel_...  25.9 us
    pallas_call x1, Pallas kernels, run_backward(): pl.pallas_call(functools.partial(mixer_backward, own_width, heads, kernel...  24 us
    all_to_all x4, waiting for transfers between devices, shard_exchange(): return lax.all_to_all(x, 'wshard', split_axis=0, concat_axis=0, tiled=True)  19.4 us
    all_to_all x4, starting transfers between devices, shard_exchange(): return lax.all_to_all(x, 'wshard', split_axis=0, concat_axis=0, tiled=True)  19.1 us
    unnamed x119, local copies, waits for them, and re-layouts  17 us
    pallas_call x2, Pallas kernels, run_weight_gradient(): pl.pallas_call(functools.partial(weight_gradient, in_rows), grid_spec=spe...  14.9 us
  transfers between devices with their start and end apart: 33, of which 9 were waited for; matrix products, arithmetic and copies ran while one was open for 16% of the time, Pallas kernels for 24%

profile of v1, /device:TPU:0, one launch (start us, length us, event | category | flops | bytes accessed | tf_op | source)
XLA Modules:
  0.0 339.7 jit_solution(5691770845518165760)
XLA Ops:
  0.8 1.2 dynamic-slice_bitcast_fusion.5
  4.4 1.0 dynamic-slice_dynamic-update-slice_fusion.1
  8.0 1.8 broadcast_in_dim.18
  9.8 4.9 %all-to-all-start = ((bf16[4,928,384]{2,1,0:T(8,128)(2,1)}), bf16[4,928,384]{2,1,0:T(8,128)(2,1)}, u32[]{:S(2)}, u32[]{:S(2)}) async-start(bf16[4,928,384]{2,1,0:T(8,128)(2,1)} %broadcast_in_dim.18), calls=%async_computation | async-start | bytes 5701632 | tf_op jit(solution)/shard_map/all_to_all | solution.py:821
  15.7 2.8 collective-permute-start.2
  18.4 2.6 collective-permute-start.3
  21.0 3.7 %constant_dynamic-slice_fusion.11 = bf16[48,6448]{0,1:T(8,128)(2,1)} fusion(bf16[384,6448]{0,1:T(8,128)(2,1)} %param.25, s32[]{:T(128)S(6)} %select_n.182), kind=kLoop, calls=%fused_computation.101 | loop fusion | bytes 1238020 | tf_op jit(solution)/shard_map/dynamic_slice | solution.py:986
  24.7 1.8 copy.93.weight_ref
  26.7 2.2 maximum_select_fusion.4.refs_0_
  29.0 24.0 %collective-permute-done.2.refs_1_ = bf16[256,1536]{1,0:T(8,128)(2,1)S(1)} collective-permute-done((bf16[256,1536]{1,0:T(8,128)(2,1)S(1)}, bf16[256,1536]{1,0:T(8,128)(2,1)S(1)}, u32[]{:S(2)}, u32[]{:S(2)}) %collective-permute-start.2) | collective-permute-done | bytes 786464 | tf_op jit(solution)/shard_map/ppermute | solution.py:815
  52.9 2.5 collective-permute-done.3.refs_2_
  57.1 2.6 collective-permute-start.7
  60.0 1.1 constant_dynamic-slice_fusion.20
  61.1 1.6 broadcast_in_dim.19
  62.7 4.1 %all-to-all-start.1 = ((bf16[4,192,1536]{2,1,0:T(8,128)(2,1)}), bf16[4,192,1536]{2,1,0:T(8,128)(2,1)S(1)}, u32[]{:S(2)}, u32[]{:S(2)}) async-start(bf16[4,192,1536]{2,1,0:T(8,128)(2,1)} %broadcast_in_dim.19), calls=%async_computation.1 | async-start | bytes 4718592 | tf_op jit(solution)/shard_map/all_to_all | solution.py:821
  67.4 1.5 collective-permute-start.4
  69.0 1.3 collective-permute-start.5
  72.8 2.4 constant_dynamic-slice_fusion.10
  75.2 19.4 %all-to-all-done.1 = bf16[4,192,1536]{2,1,0:T(8,128)(2,1)S(1)} async-done(((bf16[4,192,1536]{2,1,0:T(8,128)(2,1)}), bf16[4,192,1536]{2,1,0:T(8,128)(2,1)S(1)}, u32[]{:S(2)}, u32[]{:S(2)}) %all-to-all-start.1) | async-done | bytes 2359328 | tf_op jit(solution)/shard_map/all_to_all | solution.py:821
  94.6 3.7 %broadcast_in_dim.22 = bf16[4,768,768]{2,1,0:T(8,128)(2,1)} broadcast(bf16[768,768]{1,0:T(8,128)(2,1)} %constant_dynamic-slice_fusion.10), dimensions={1,2} | broadcast | bytes 5898240 | tf_op jit(solution)/shard_map/broadcast_in_dim | solution.py:954
  98.3 5.0 %all-to-all-start.2 = ((bf16[4,768,768]{2,1,0:T(8,128)(2,1)}), bf16[4,768,768]{2,1,0:T(8,128)(2,1)}, u32[]{:S(2)}, u32[]{:S(2)}) async-start(bf16[4,768,768]{2,1,0:T(8,128)(2,1)} %broadcast_in_dim.22), calls=%async_computation.2 | async-start | bytes 9437184 | tf_op jit(solution)/shard_map/all_to_all | solution.py:821
  103.3 7.4 %collective-permute-done.5 = bf16[256,1536]{1,0:T(8,128)(2,1)} collective-permute-done((bf16[256,1536]{1,0:T(8,128)(2,1)}, bf16[256,1536]{1,0:T(8,128)(2,1)}, u32[]{:S(2)}, u32[]{:S(2)}) %collective-permute-start.5) | collective-permute-done | bytes 786464 | tf_op jit(solution)/shard_map/ppermute | solution.py:815
  110.7 1.3 collective-permute-start.10
  112.9 1.2 broadcast_select_fusion.1.refs_3_
  114.1 25.9 %mixer_forward.1 = (bf16[1808,1536]{1,0:T(8,128)(2,1)}, bf16[4,256,1536]{2,1,0:T(8,128)(2,1)}, f32[768,1024]{1,0:T(8,128)}, bf16[1024,1024]{1,0:T(8,128)(2,1)}, ...) custom-call(s32[5]{0:T(128)S(1)} %pad_add_fusion.order_ref, ...), custom_call_target="tpu_custom_call" | custom-call | flops 22749904896 | bytes 33554432 | tf_op jit(solution)/shard_map/mixer_forward/pallas_call | solution.py:438
  140.7 1.9 copy-done
  142.6 7.1 %gate_statistics.1 = (bf16[4,256,1536]{2,1,0:T(8,128)(2,1)S(1)}, f32[768,1024]{1,0:T(8,128)S(1)}, f32[8,1024]{1,0:T(8,128)S(1)}) custom-call(s32[5]{0:T(128)S(1)} %pad_add_fusion.order_ref, f32[768,1024]{1,0:T(8,128)S(1)} %copy-done, bf16[768,1024]{1,0:T(8,128)(2,1)S(1)} %get-tuple-element.159.sent_ref, bf16[256,1536]{1,0:T(8,128)(2,1)} %maximum_select_fusion.4.refs_0_, ...), custom_call_target="tpu_custom_call" | custom-call | flops 2415919104 | bytes 16777216 | tf_op jit(solution)/shard_map/gate_statistics/pallas_call | solution.py:491
  149.7 1.7 copy-done.10
  151.4 5.5 %collective-permute-start.11 = (f32[2,1024]{1,0:T(2,128)S(1)}, f32[2,1024]{1,0:T(2,128)S(1)}, u32[]{:S(2)}, u32[]{:S(2)}) collective-permute-start(f32[2,1024]{1,0:T(2,128)S(1)} %slice.123), channel_id=1, source_target_pairs={{0,2},{1,3},{2,0},{3,1},{4,6},{5,7},{6,4},{7,5},{8,10},{9,11},{10,... | collective-permute-start | bytes 24584 | tf_op jit(solution)/shard_map/ppermute | solution.py:815
  156.9 2.4 collective-permute-start.13
  159.2 2.2 collective-permute-done.12
  162.4 4.5 %gate_backward.1 = (bf16[768,1024]{1,0:T(8,128)(2,1)S(1)}, bf16[768,1024]{1,0:T(8,128)(2,1)S(1)}, bf16[768,1024]{1,0:T(8,128)(2,1)S(1)}) custom-call(s32[5]{0:T(128)S(1)} %pad_add_fusion.order_ref, f32[768,1024]{1,0:T(8,128)S(1)} %copy-done.1, bf16[768,1024]{1,0:T(8,128)(2,1)S(1)} %get-tuple-element.159.sent_ref, ...), custom_call_target="tpu_custom_call" | custom-call | flops 15728640 | bytes 11010048 | tf_op jit(solution)/shard_map/gate_backward/pallas_call | solution.py:532
  166.9 1.1 copy-done.3
  168.1 1.1 copy-done.11
  169.2 1.1 fusion.44
  170.3 4.7 %convolution_convert_fusion = bf16[768,1536]{1,0:T(8,128)(2,1)S(1)} fusion(bf16[768,1024]{1,0:T(8,128)(2,1)S(1)} %get-tuple-element.211, bf16[1024,1536]{1,0:T(8,128)(2,1)} %bitcast.82), kind=kOutput, calls=%fused_computation.3 | convolution fusion | flops 2417098752 | bytes 7077888 | tf_op jit(solution)/shard_map/dot_general | solution.py:1055
  175.2 6.6 %weight_gradient.2 = (bf16[16,48,768]{2,1,0:T(8,128)(2,1)}, bf16[16,48,768]{2,1,0:T(8,128)(2,1)}) custom-call(s32[1]{0:T(128)} %bitcast.core_ref, bf16[1024,1536]{1,0:T(8,128)(2,1)} %bitcast.83, bf16[768,1024]{1,0:T(8,128)(2,1)} %copy-done.3), custom_call_target="tpu_custom_call" | custom-call | flops 1048576 | bytes 131072 | tf_op jit(solution)/shard_map/weight_gradient/pallas_call | solution.py:668
  182.4 2.8 collective-permute-start.15
  185.2 1.5 collective-permute-start.16
  186.6 24.0 %mixer_backward.1 = (bf16[1040,1024]{1,0:T(8,128)(2,1)}, f32[8,1024]{1,0:T(8,128)}, f32[3,16,128]{2,1,0:T(8,128)}) custom-call(s32[5]{0:T(128)} %copy-done.9, bf16[768,1024]{1,0:T(8,128)(2,1)} %copy-done.11, f32[1024,1024]{1,0:T(8,128)} %get-tuple-element.178.conv_ref, bf16[1024,1024]{1,0:T(8,128)(2,1)} %get-tuple-element.179.values_ref, ...), custom_call_target="tpu_custom_call" | custom-call | flops 34359738368 | bytes 25165824 | tf_op jit(solution)/shard_map/mixer_backward/pallas_call | solution.py:585
  210.7 8.3 %weight_gradient.3 = (bf16[16,48,1040]{2,1,0:T(8,128)(2,1)}, bf16[16,48,1040]{2,1,0:T(8,128)(2,1)}) custom-call(s32[1]{0:T(128)} %bitcast.core_ref, bf16[1024,1536]{1,0:T(8,128)(2,1)} %bitcast.84, bf16[1040,1024]{1,0:T(8,128)(2,1)} %get-tuple-element.197.grad_ref.drest_ref), custom_call_target="tpu_custom_call" | custom-call | flops 1048576 | bytes 131072 | tf_op jit(solution)/shard_map/weight_gradient/pallas_call | solution.py:668
  220.5 1.1 pad_maximum_fusion.3
  224.8 12.3 %token_gradient.1 = (bf16[256,1536]{1,0:T(8,128)(2,1)}, bf16[256,1536]{1,0:T(8,128)(2,1)}, bf16[256,1536]{1,0:T(8,128)(2,1)}, bf16[256,1536]{1,0:T(8,128)(2,1)}) custom-call(bf16[768,1024]{1,0:T(8,128)(2,1)} %copy-done.3, bf16[1040,1024]{1,0:T(8,128)(2,1)} %get-tuple-element.197.grad_ref.drest_ref, bf16[1808,1536]{1,0:T(8,128)(2,1)} %get-tuple-element.198.weight_ref), custom_call_target="tpu_custom_call" | custom-call | flops 5687476224 | bytes 12582912 | tf_op jit(solution)/shard_map/token_gradient/pallas_call | solution.py:619
  237.1 4.1 %collective-permute-start.22 = (bf16[256,1536]{1,0:T(8,128)(2,1)}, bf16[256,1536]{1,0:T(8,128)(2,1)}, u32[]{:S(2)}, u32[]{:S(2)}) collective-permute-start(bf16[256,1536]{1,0:T(8,128)(2,1)} %get-tuple-element.206), channel_id=1, source_target_pairs={{0,2},{1,3},{6,4},{7,5},{8,10},{9,11},{14,12},{15,13},{16,18},{17,... | collective-permute-start | bytes 2359304 | tf_op jit(solution)/shard_map/ppermute | solution.py:815
  241.2 1.6 collective-permute-start.23
  242.9 2.0 add_convert_fusion
  244.9 2.2 pad_maximum_fusion
  247.1 5.1 %all-to-all-start.3 = ((bf16[4,192,2704]{2,1,0:T(8,128)(2,1)}), bf16[4,192,2704]{2,1,0:T(8,128)(2,1)}, u32[]{:S(2)}, u32[]{:S(2)}) async-start(bf16[4,192,2704]{2,1,0:T(8,128)(2,1)} %pad_maximum_fusion), calls=%async_computation.3 | async-start | bytes 8650752 | tf_op jit(solution)/shard_map/all_to_all | solution.py:821
  252.2 5.3 %collective-permute-done.22 = bf16[256,1536]{1,0:T(8,128)(2,1)} collective-permute-done((bf16[256,1536]{1,0:T(8,128)(2,1)}, bf16[256,1536]{1,0:T(8,128)(2,1)}, u32[]{:S(2)}, u32[]{:S(2)}) %collective-permute-start.22) | collective-permute-done | bytes 786464 | tf_op jit(solution)/shard_map/ppermute | solution.py:815
  257.6 3.8 %collective-permute-start.24 = (bf16[256,1536]{1,0:T(8,128)(2,1)}, bf16[256,1536]{1,0:T(8,128)(2,1)S(1)}, u32[]{:S(2)}, u32[]{:S(2)}) collective-permute-start(bf16[256,1536]{1,0:T(8,128)(2,1)} %get-tuple-element.207), channel_id=1, source_target_pairs={{0,2},{1,3},{2,0},{3,1},{4,6},{5,7},{6,4},{7,5},{8,10},{9,11},{10,... | collective-permute-start | bytes 2359304 | tf_op jit(solution)/shard_map/ppermute | solution.py:815
  261.4 1.7 add_convert_fusion.3
  263.0 1.0 collective-permute-start.25
  264.0 29.5 %collective-permute-done.24 = bf16[256,1536]{1,0:T(8,128)(2,1)S(1)} collective-permute-done((bf16[256,1536]{1,0:T(8,128)(2,1)}, bf16[256,1536]{1,0:T(8,128)(2,1)S(1)}, u32[]{:S(2)}, u32[]{:S(2)}) %collective-permute-start.24) | collective-permute-done | bytes 786464 | tf_op jit(solution)/shard_map/ppermute | solution.py:815
  294.9 3.8 %fusion.47 = f32[256,768]{1,0:T(8,128)S(1)} fusion(bf16[3072,256]{1,0:T(8,128)(2,1)S(1)} %bitcast.97, bf16[3072,768]{1,0:T(8,128)(2,1)} %bitcast.22), kind=kOutput, calls=%fused_computation.162 | convolution fusion | flops 1207959552 | bytes 7077888 | tf_op jit(solution)/shard_map/dot_general | solution.py:35
  298.7 3.8 %fusion.48 = f32[256,768]{1,0:T(8,128)S(1)} fusion(bf16[3072,256]{1,0:T(8,128)(2,1)S(1)} %bitcast.98, bf16[3072,768]{1,0:T(8,128)(2,1)} %collective-permute-done.21), kind=kOutput, calls=%fused_computation.163 | convolution fusion | flops 1207959552 | bytes 7077888 | tf_op jit(solution)/shard_map/dot_general | solution.py:35
  302.6 3.1 convert_reduce_fusion
  307.8 3.5 %all-to-all-start.4 = ((bf16[4,48,2064]{2,1,0:T(8,128)(2,1)}), bf16[4,48,2064]{2,1,0:T(8,128)(2,1)S(1)}, u32[]{:S(2)}, u32[]{:S(2)}) async-start(bf16[4,48,2064]{2,1,0:T(8,128)(2,1)} %pad_maximum_fusion.4), calls=%async_computation.4 | async-start | bytes 1671168 | tf_op jit(solution)/shard_map/all_to_all | solution.py:828
  311.3 2.2 convert_add_fusion.1
  315.4 2.8 fusion.9
  318.3 1.4 add_multiply_fusion.2
  320.2 2.5 fusion.4
  322.7 8.9 %all-to-all-done.4.found_ref = bf16[4,48,2064]{2,1,0:T(8,128)(2,1)S(1)} async-done(((bf16[4,48,2064]{2,1,0:T(8,128)(2,1)}), bf16[4,48,2064]{2,1,0:T(8,128)(2,1)S(1)}, u32[]{:S(2)}, u32[]{:S(2)}) %all-to-all-start.4) | async-done | bytes 792608 | tf_op jit(solution)/shard_map/all_to_all | solution.py:828
  332.3 1.3 copy-done.5
  333.6 3.3 finish_weight.1
  (254 shorter events, 28.0 us)
Async XLA Ops:
  0.7 5.7 %slice-start = ((bf16[384,6448]{0,1:T(8,128)(2,1)}), bf16[384,48]{0,1:T(8,128)(2,1)S(1)}, s32[]{:S(2)}) async-start(bf16[384,6448]{0,1:T(8,128)(2,1)} %param.25), calls=%async_computation.5 | async-start | bytes 73728 | tf_op jit(solution)/shard_map/slice | solution.py:890
  0.7 5.8 %copy-start.39 = (bf16[5,832]{1,0:T(8,128)(2,1)S(1)}, bf16[5,832]{1,0:T(8,128)(2,1)}, u32[]{:S(2)}) copy-start(bf16[5,832]{1,0:T(8,128)(2,1)} %param.28) | copy-start | bytes 24964
  0.7 5.9 %copy-start.48 = (bf16[3,12]{1,0:T(4,128)(2,1)S(1)}, bf16[3,12]{1,0:T(4,128)(2,1)}, u32[]{:S(2)}) copy-start(bf16[3,12]{1,0:T(4,128)(2,1)} %param.31) | copy-start | bytes 220
  0.7 5.9 %copy-start.44 = (bf16[384]{0:T(512)(128)(2,1)S(1)}, bf16[384]{0:T(512)(128)(2,1)}, u32[]{:S(2)}) copy-start(bf16[384]{0:T(512)(128)(2,1)} %param.22) | copy-start | bytes 2308
  0.7 5.9 %copy-start.43 = (bf16[768]{0:T(1024)(128)(2,1)S(1)}, bf16[768]{0:T(1024)(128)(2,1)}, u32[]{:S(2)}) copy-start(bf16[768]{0:T(1024)(128)(2,1)} %param.34) | copy-start | bytes 4612
  1.9 5.9 %collective-permute-start = (bf16[128,1536]{1,0:T(8,128)(2,1)S(1)}, bf16[128,1536]{1,0:T(8,128)(2,1)S(1)}, u32[]{:S(2)}, u32[]{:S(2)}) collective-permute-start(bf16[128,1536]{1,0:T(8,128)(2,1)S(1)} %get-tuple-element.288), channel_id=1, source_target_pairs={{0,1},{1,0},{2,3},{3,2},{4,5},{5,4},{6,7},{7,6},{8,9},{9,8},{10,11... | collective-permute-start | bytes 1179656 | tf_op jit(solution)/shard_map/ppermute | solution.py:809
  8.0 10.5 %copy-start.6 = (bf16[256,1536]{1,0:T(8,128)(2,1)}, bf16[256,1536]{1,0:T(8,128)(2,1)S(1)}, u32[]{:S(2)}) copy-start(bf16[256,1536]{1,0:T(8,128)(2,1)S(1)} %maximum_select_fusion.3.refs_0_) | copy-start | bytes 2359300
  9.8 4.9 %copy-start.19 = (bf16[2,128,1536]{2,1,0:T(8,128)(2,1)S(1)}, bf16[2,128,1536]{2,1,0:T(8,128)(2,1)}, u32[]{:S(2)}) copy-start(bf16[2,128,1536]{2,1,0:T(8,128)(2,1)} %param.21) | copy-start | bytes 2359300
  9.8 45.7 %all-to-all-start = ((bf16[4,928,384]{2,1,0:T(8,128)(2,1)}), bf16[4,928,384]{2,1,0:T(8,128)(2,1)}, u32[]{:S(2)}, u32[]{:S(2)}) async-start(bf16[4,928,384]{2,1,0:T(8,128)(2,1)} %broadcast_in_dim.18), calls=%async_computation | async-start | bytes 5701632 | tf_op jit(solution)/shard_map/all_to_all | solution.py:821
  15.5 11.3 %collective-permute-start.1 = (bf16[128,1536]{1,0:T(8,128)(2,1)}, bf16[128,1536]{1,0:T(8,128)(2,1)}, u32[]{:S(2)}, u32[]{:S(2)}) collective-permute-start(bf16[128,1536]{1,0:T(8,128)(2,1)} %get-tuple-element.286), channel_id=1, source_target_pairs={{0,1},{1,0},{2,3},{3,2},{4,5},{5,4},{6,7},{7,6},{8,9},{9,8},{10,11... | collective-permute-start | bytes 1179656 | tf_op jit(solution)/shard_map/ppermute | solution.py:809
  15.7 37.3 %collective-permute-start.2 = (bf16[256,1536]{1,0:T(8,128)(2,1)S(1)}, bf16[256,1536]{1,0:T(8,128)(2,1)S(1)}, u32[]{:S(2)}, u32[]{:S(2)}) collective-permute-start(bf16[256,1536]{1,0:T(8,128)(2,1)S(1)} %maximum_select_fusion.3.refs_0_), channel_id=1, source_target_pairs={{0,2},{1,3},{2,0},{3,1},{4,6},{5,7},{6,4},{7,5},{8,10},{9,11},{10,... | collective-permute-start | bytes 2359304 | tf_op jit(solution)/shard_map/ppermute | solution.py:815
  18.4 37.0 %collective-permute-start.3 = (bf16[256,1536]{1,0:T(8,128)(2,1)S(1)}, bf16[256,1536]{1,0:T(8,128)(2,1)S(1)}, u32[]{:S(2)}, u32[]{:S(2)}) collective-permute-start(bf16[256,1536]{1,0:T(8,128)(2,1)S(1)} %maximum_select_fusion.3.refs_0_), channel_id=1, source_target_pairs={{0,4},{1,5},{2,6},{3,7},{4,0},{5,1},{6,2},{7,3},{8,12},{9,13},{10,... | collective-permute-start | bytes 2359304 | tf_op jit(solution)/shard_map/ppermute | solution.py:815
  26.7 135.6 %copy-start.9 = (s32[5]{0:T(128)}, s32[5]{0:T(128)S(1)}, u32[]{:S(2)}) copy-start(s32[5]{0:T(128)S(1)} %pad_add_fusion.order_ref) | copy-start | bytes 64
  52.9 9.7 %copy-start.12 = (bf16[256,1536]{1,0:T(8,128)(2,1)}, bf16[256,1536]{1,0:T(8,128)(2,1)S(1)}, u32[]{:S(2)}) copy-start(bf16[256,1536]{1,0:T(8,128)(2,1)S(1)} %collective-permute-done.2.refs_1_) | copy-start | bytes 2359300
  55.5 7.2 %copy-start.14 = (bf16[256,1536]{1,0:T(8,128)(2,1)}, bf16[256,1536]{1,0:T(8,128)(2,1)S(1)}, u32[]{:S(2)}) copy-start(bf16[256,1536]{1,0:T(8,128)(2,1)S(1)} %collective-permute-done.3.refs_2_) | copy-start | bytes 2359300
  56.3 57.8 %collective-permute-start.8 = (bf16[4,928,384]{2,1,0:T(8,128)(2,1)}, bf16[4,928,384]{2,1,0:T(8,128)(2,1)}, u32[]{:S(2)}, u32[]{:S(2)}) collective-permute-start(bf16[4,928,384]{2,1,0:T(8,128)(2,1)} %all-to-all-done.refs_7_), channel_id=1, source_target_pairs={{0,1},{1,0},{2,3},{3,2},{4,5},{5,4},{6,7},{7,6},{8,9},{9,8},{10,11... | collective-permute-start | bytes 8552456 | tf_op jit(solution)/shard_map/ppermute | solution.py:809
  56.3 10.9 %copy-start.36 = (bf16[1,4,16,384]{3,1,2,0:T(4,128)(2,1)}, bf16[1,4,16,384]{3,1,2,0:T(4,128)(2,1)S(1)}, u32[]{:S(2)}) copy-start(bf16[1,4,16,384]{3,1,2,0:T(4,128)(2,1)S(1)} %copy.94) | copy-start | bytes 147460
  56.6 54.0 %collective-permute-start.6 = (bf16[256,1536]{1,0:T(8,128)(2,1)}, bf16[256,1536]{1,0:T(8,128)(2,1)}, u32[]{:S(2)}, u32[]{:S(2)}) collective-permute-start(bf16[256,1536]{1,0:T(8,128)(2,1)} %maximum_select_fusion.4.refs_0_), channel_id=1, source_target_pairs={{0,2},{1,3},{2,0},{3,1},{4,6},{5,7},{6,4},{7,5},{8,10},{9,11},{10,... | collective-permute-start | bytes 2359304 | tf_op jit(solution)/shard_map/ppermute | solution.py:815
  57.1 53.5 %collective-permute-start.7 = (bf16[256,1536]{1,0:T(8,128)(2,1)}, bf16[256,1536]{1,0:T(8,128)(2,1)}, u32[]{:S(2)}, u32[]{:S(2)}) collective-permute-start(bf16[256,1536]{1,0:T(8,128)(2,1)} %maximum_select_fusion.4.refs_0_), channel_id=1, source_target_pairs={{0,4},{1,5},{2,6},{3,7},{4,0},{5,1},{6,2},{7,3},{8,12},{9,13},{10,... | collective-permute-start | bytes 2359304 | tf_op jit(solution)/shard_map/ppermute | solution.py:815
  62.7 31.9 %all-to-all-start.1 = ((bf16[4,192,1536]{2,1,0:T(8,128)(2,1)}), bf16[4,192,1536]{2,1,0:T(8,128)(2,1)S(1)}, u32[]{:S(2)}, u32[]{:S(2)}) async-start(bf16[4,192,1536]{2,1,0:T(8,128)(2,1)} %broadcast_in_dim.19), calls=%async_computation.1 | async-start | bytes 4718592 | tf_op jit(solution)/shard_map/all_to_all | solution.py:821
  67.1 47.0 %copy-start.8 = (f32[16,128]{1,0:T(8,128)}, f32[16,128]{1,0:T(8,128)S(1)}, u32[]{:S(2)}) copy-start(f32[16,128]{1,0:T(8,128)S(1)} %pad.31.refs_6_.head_ref) | copy-start | bytes 24580
  67.4 35.9 %collective-permute-start.4 = (bf16[256,1536]{1,0:T(8,128)(2,1)}, bf16[256,1536]{1,0:T(8,128)(2,1)}, u32[]{:S(2)}, u32[]{:S(2)}) collective-permute-start(bf16[256,1536]{1,0:T(8,128)(2,1)} %copy-done.6), channel_id=1, source_target_pairs={{2,4},{3,5},{4,2},{5,3},{10,12},{11,13},{12,10},{13,11},{18,20},{1... | collective-permute-start | bytes 2359304 | tf_op jit(solution)/shard_map/ppermute | solution.py:815
  69.0 41.7 %collective-permute-start.5 = (bf16[256,1536]{1,0:T(8,128)(2,1)}, bf16[256,1536]{1,0:T(8,128)(2,1)}, u32[]{:S(2)}, u32[]{:S(2)}) collective-permute-start(bf16[256,1536]{1,0:T(8,128)(2,1)} %copy-done.14), channel_id=1, source_target_pairs={{2,0},{3,1},{4,6},{5,7},{10,8},{11,9},{12,14},{13,15},{18,16},{19,... | collective-permute-start | bytes 2359304 | tf_op jit(solution)/shard_map/ppermute | solution.py:815
  72.1 90.3 %copy-start.2 = (f32[8,1024]{0,1:T(8,128)}, f32[8,1024]{0,1:T(8,128)S(1)}, u32[]{:S(2)}) copy-start(f32[8,1024]{0,1:T(8,128)S(1)} %copy.85) | copy-start | bytes 98308
  98.3 70.9 %all-to-all-start.2 = ((bf16[4,768,768]{2,1,0:T(8,128)(2,1)}), bf16[4,768,768]{2,1,0:T(8,128)(2,1)}, u32[]{:S(2)}, u32[]{:S(2)}) async-start(bf16[4,768,768]{2,1,0:T(8,128)(2,1)} %broadcast_in_dim.22), calls=%async_computation.2 | async-start | bytes 9437184 | tf_op jit(solution)/shard_map/all_to_all | solution.py:821
  103.3 10.9 %copy-start.7 = (bf16[256,1536]{1,0:T(8,128)(2,1)S(1)}, bf16[256,1536]{1,0:T(8,128)(2,1)}, u32[]{:S(2)}) copy-start(bf16[256,1536]{1,0:T(8,128)(2,1)} %copy-done.6) | copy-start | bytes 2359300
  103.3 10.9 %copy-start.13 = (bf16[256,1536]{1,0:T(8,128)(2,1)S(1)}, bf16[256,1536]{1,0:T(8,128)(2,1)}, u32[]{:S(2)}) copy-start(bf16[256,1536]{1,0:T(8,128)(2,1)} %copy-done.12) | copy-start | bytes 2359300
  103.3 10.8 %copy-start.15 = (bf16[256,1536]{1,0:T(8,128)(2,1)S(1)}, bf16[256,1536]{1,0:T(8,128)(2,1)}, u32[]{:S(2)}) copy-start(bf16[256,1536]{1,0:T(8,128)(2,1)} %copy-done.14) | copy-start | bytes 2359300
  110.7 29.4 %collective-permute-start.10 = (bf16[256,1536]{1,0:T(8,128)(2,1)}, bf16[256,1536]{1,0:T(8,128)(2,1)S(1)}, u32[]{:S(2)}, u32[]{:S(2)}) collective-permute-start(bf16[256,1536]{1,0:T(8,128)(2,1)} %collective-permute-done.7.refs_2_), channel_id=1, source_target_pairs={{2,0},{3,1},{4,6},{5,7},{10,8},{11,9},{12,14},{13,15},{18,16},{19,... | collective-permute-start | bytes 2359304 | tf_op jit(solution)/shard_map/ppermute | solution.py:815
  112.0 28.1 %collective-permute-start.9 = (bf16[256,1536]{1,0:T(8,128)(2,1)}, bf16[256,1536]{1,0:T(8,128)(2,1)S(1)}, u32[]{:S(2)}, u32[]{:S(2)}) collective-permute-start(bf16[256,1536]{1,0:T(8,128)(2,1)} %maximum_select_fusion.4.refs_0_), channel_id=1, source_target_pairs={{2,4},{3,5},{4,2},{5,3},{10,12},{11,13},{12,10},{13,11},{18,20},{1... | collective-permute-start | bytes 2359304 | tf_op jit(solution)/shard_map/ppermute | solution.py:815
  142.6 19.8 %copy-start.1 = (f32[768,1024]{1,0:T(8,128)S(1)}, f32[768,1024]{1,0:T(8,128)}, u32[]{:S(2)}) copy-start(f32[768,1024]{1,0:T(8,128)} %get-tuple-element.158.gates_ref) | copy-start | bytes 9437188
  151.4 7.8 %collective-permute-start.11 = (f32[2,1024]{1,0:T(2,128)S(1)}, f32[2,1024]{1,0:T(2,128)S(1)}, u32[]{:S(2)}, u32[]{:S(2)}) collective-permute-start(f32[2,1024]{1,0:T(2,128)S(1)} %slice.123), channel_id=1, source_target_pairs={{0,2},{1,3},{2,0},{3,1},{4,6},{5,7},{6,4},{7,5},{8,10},{9,11},{10,... | collective-permute-start | bytes 24584 | tf_op jit(solution)/shard_map/ppermute | solution.py:815
  156.9 4.5 %collective-permute-start.12 = (f32[2,1024]{1,0:T(2,128)S(1)}, f32[2,1024]{1,0:T(2,128)S(1)}, u32[]{:S(2)}, u32[]{:S(2)}) collective-permute-start(f32[2,1024]{1,0:T(2,128)S(1)} %slice.123), channel_id=1, source_target_pairs={{0,4},{1,5},{2,6},{3,7},{4,0},{5,1},{6,2},{7,3},{8,12},{9,13},{10,... | collective-permute-start | bytes 24584 | tf_op jit(solution)/shard_map/ppermute | solution.py:815
  156.9 5.4 %collective-permute-start.13 = (f32[2,1024]{1,0:T(2,128)S(1)}, f32[2,1024]{1,0:T(2,128)S(1)}, u32[]{:S(2)}, u32[]{:S(2)}) collective-permute-start(f32[2,1024]{1,0:T(2,128)S(1)} %slice.123), channel_id=1, source_target_pairs={{0,6},{1,7},{2,4},{3,5},{4,2},{5,3},{6,0},{7,1},{8,14},{9,15},{10,... | collective-permute-start | bytes 24584 | tf_op jit(solution)/shard_map/ppermute | solution.py:815
  181.7 37.3 %collective-permute-start.18 = (bf16[4,4,48,768]{3,2,1,0:T(8,128)(2,1)}, bf16[4,4,48,768]{3,2,1,0:T(8,128)(2,1)S(1)}, u32[]{:S(2)}, u32[]{:S(2)}) collective-permute-start(bf16[4,4,48,768]{3,2,1,0:T(8,128)(2,1)} %bitcast.115), channel_id=1, source_target_pairs={{0,1},{1,0},{2,3},{3,2},{4,5},{5,4},{6,7},{7,6},{8,9},{9,8},{10,11... | collective-permute-start | bytes 3538952 | tf_op jit(solution)/shard_map/ppermute | solution.py:809
  181.7 37.3 %collective-permute-start.17 = (bf16[4,96,1536]{2,1,0:T(8,128)(2,1)S(1)}, bf16[4,96,1536]{2,1,0:T(8,128)(2,1)S(1)}, u32[]{:S(2)}, u32[]{:S(2)}) collective-permute-start(bf16[4,96,1536]{2,1,0:T(8,128)(2,1)S(1)} %get-tuple-element.268), channel_id=1, source_target_pairs={{0,1},{1,0},{2,3},{3,2},{4,5},{5,4},{6,7},{7,6},{8,9},{9,8},{10,11... | collective-permute-start | bytes 3538952 | tf_op jit(solution)/shard_map/ppermute | solution.py:809
  182.2 36.7 %collective-permute-start.14 = (bf16[768,256]{1,0:T(8,128)(2,1)}, bf16[768,256]{1,0:T(8,128)(2,1)S(1)}, u32[]{:S(2)}, u32[]{:S(2)}) collective-permute-start(bf16[768,256]{1,0:T(8,128)(2,1)} %get-tuple-element.280), channel_id=1, source_target_pairs={{0,2},{1,3},{2,0},{3,1},{4,6},{5,7},{6,4},{7,5},{8,10},{9,11},{10,... | collective-permute-start | bytes 1179656 | tf_op jit(solution)/shard_map/ppermute | solution.py:815
  182.4 36.6 %collective-permute-start.15 = (bf16[768,256]{1,0:T(8,128)(2,1)}, bf16[768,256]{1,0:T(8,128)(2,1)S(1)}, u32[]{:S(2)}, u32[]{:S(2)}) collective-permute-start(bf16[768,256]{1,0:T(8,128)(2,1)} %get-tuple-element.279), channel_id=1, source_target_pairs={{0,4},{1,5},{2,6},{3,7},{4,0},{5,1},{6,2},{7,3},{8,12},{9,13},{10,... | collective-permute-start | bytes 1179656 | tf_op jit(solution)/shard_map/ppermute | solution.py:815
  185.2 33.8 %collective-permute-start.16 = (bf16[768,256]{1,0:T(8,128)(2,1)}, bf16[768,256]{1,0:T(8,128)(2,1)S(1)}, u32[]{:S(2)}, u32[]{:S(2)}) collective-permute-start(bf16[768,256]{1,0:T(8,128)(2,1)} %get-tuple-element.278), channel_id=1, source_target_pairs={{0,6},{1,7},{2,4},{3,5},{4,2},{5,3},{6,0},{7,1},{8,14},{9,15},{10,... | collective-permute-start | bytes 1179656 | tf_op jit(solution)/shard_map/ppermute | solution.py:815
  219.0 18.1 %collective-permute-start.21 = (bf16[3072,768]{1,0:T(8,128)(2,1)}, bf16[3072,768]{1,0:T(8,128)(2,1)}, u32[]{:S(2)}, u32[]{:S(2)}) collective-permute-start(bf16[3072,768]{1,0:T(8,128)(2,1)} %bitcast.22), channel_id=1, source_target_pairs={{0,1},{1,0},{2,3},{3,2},{4,5},{5,4},{6,7},{7,6},{8,9},{9,8},{10,11... | collective-permute-start | bytes 14155784 | tf_op jit(solution)/shard_map/ppermute | solution.py:809
  220.1 17.0 %collective-permute-start.20 = (bf16[4,4,48,1040]{3,2,1,0:T(8,128)(2,1)}, bf16[4,4,48,1040]{3,2,1,0:T(8,128)(2,1)}, u32[]{:S(2)}, u32[]{:S(2)}) collective-permute-start(bf16[4,4,48,1040]{3,2,1,0:T(8,128)(2,1)} %bitcast.114), channel_id=1, source_target_pairs={{0,1},{1,0},{2,3},{3,2},{4,5},{5,4},{6,7},{7,6},{8,9},{9,8},{10,11... | collective-permute-start | bytes 4792328 | tf_op jit(solution)/shard_map/ppermute | solution.py:809
  224.2 12.9 %collective-permute-start.19 = (f32[5156]{0:T(1024)S(1)}, f32[5156]{0:T(1024)S(1)}, u32[]{:S(2)}, u32[]{:S(2)}) collective-permute-start(f32[5156]{0:T(1024)S(1)} %constant_dynamic-update-slice_fusion.2), channel_id=1, source_target_pairs={{0,1},{1,0},{2,3},{3,2},{4,5},{5,4},{6,7},{7,6},{8,9},{9,8},{10,11... | collective-permute-start | bytes 61880 | tf_op jit(solution)/shard_map/ppermute | solution.py:809
  224.8 18.1 %copy-start.23 = (bf16[16,48,1040]{2,1,0:T(8,128)(2,1)S(1)}, bf16[16,48,1040]{2,1,0:T(8,128)(2,1)}, u32[]{:S(2)}) copy-start(bf16[16,48,1040]{2,1,0:T(8,128)(2,1)} %get-tuple-element.183) | copy-start | bytes 4792324
  237.1 20.4 %collective-permute-start.22 = (bf16[256,1536]{1,0:T(8,128)(2,1)}, bf16[256,1536]{1,0:T(8,128)(2,1)}, u32[]{:S(2)}, u32[]{:S(2)}) collective-permute-start(bf16[256,1536]{1,0:T(8,128)(2,1)} %get-tuple-element.206), channel_id=1, source_target_pairs={{0,2},{1,3},{6,4},{7,5},{8,10},{9,11},{14,12},{15,13},{16,18},{17,... | collective-permute-start | bytes 2359304 | tf_op jit(solution)/shard_map/ppermute | solution.py:815
  241.2 16.4 %collective-permute-start.23 = (bf16[256,1536]{1,0:T(8,128)(2,1)}, bf16[256,1536]{1,0:T(8,128)(2,1)}, u32[]{:S(2)}, u32[]{:S(2)}) collective-permute-start(bf16[256,1536]{1,0:T(8,128)(2,1)} %get-tuple-element.206), channel_id=1, source_target_pairs={{2,4},{3,5},{4,2},{5,3},{10,12},{11,13},{12,10},{13,11},{18,20},{1... | collective-permute-start | bytes 2359304 | tf_op jit(solution)/shard_map/ppermute | solution.py:815
  247.1 55.5 %all-to-all-start.3 = ((bf16[4,192,2704]{2,1,0:T(8,128)(2,1)}), bf16[4,192,2704]{2,1,0:T(8,128)(2,1)}, u32[]{:S(2)}, u32[]{:S(2)}) async-start(bf16[4,192,2704]{2,1,0:T(8,128)(2,1)} %pad_maximum_fusion), calls=%async_computation.3 | async-start | bytes 8650752 | tf_op jit(solution)/shard_map/all_to_all | solution.py:821
  257.6 36.0 %collective-permute-start.24 = (bf16[256,1536]{1,0:T(8,128)(2,1)}, bf16[256,1536]{1,0:T(8,128)(2,1)S(1)}, u32[]{:S(2)}, u32[]{:S(2)}) collective-permute-start(bf16[256,1536]{1,0:T(8,128)(2,1)} %get-tuple-element.207), channel_id=1, source_target_pairs={{0,2},{1,3},{2,0},{3,1},{4,6},{5,7},{6,4},{7,5},{8,10},{9,11},{10,... | collective-permute-start | bytes 2359304 | tf_op jit(solution)/shard_map/ppermute | solution.py:815
  261.4 32.2 %copy-start.31 = (bf16[768,256]{1,0:T(8,128)(2,1)S(1)}, bf16[768,256]{1,0:T(8,128)(2,1)}, u32[]{:S(2)}) copy-start(bf16[768,256]{1,0:T(8,128)(2,1)} %copy-done.30) | copy-start | bytes 1179652
  261.4 32.3 %copy-start.33 = (bf16[768,256]{1,0:T(8,128)(2,1)S(1)}, bf16[768,256]{1,0:T(8,128)(2,1)}, u32[]{:S(2)}) copy-start(bf16[768,256]{1,0:T(8,128)(2,1)} %copy-done.32) | copy-start | bytes 1179652
  261.4 32.3 %copy-start.35 = (bf16[768,256]{1,0:T(8,128)(2,1)S(1)}, bf16[768,256]{1,0:T(8,128)(2,1)}, u32[]{:S(2)}) copy-start(bf16[768,256]{1,0:T(8,128)(2,1)} %copy-done.34) | copy-start | bytes 1179652
  263.0 39.6 %collective-permute-start.25 = (bf16[256,1536]{1,0:T(8,128)(2,1)S(1)}, bf16[256,1536]{1,0:T(8,128)(2,1)}, u32[]{:S(2)}, u32[]{:S(2)}) collective-permute-start(bf16[256,1536]{1,0:T(8,128)(2,1)S(1)} %add_convert_fusion.3), channel_id=1, source_target_pairs={{0,4},{1,5},{2,6},{3,7},{4,0},{5,1},{6,2},{7,3},{8,12},{9,13},{10,... | collective-permute-start | bytes 2359304 | tf_op jit(solution)/shard_map/ppermute | solution.py:815
  307.8 23.7 %all-to-all-start.4 = ((bf16[4,48,2064]{2,1,0:T(8,128)(2,1)}), bf16[4,48,2064]{2,1,0:T(8,128)(2,1)S(1)}, u32[]{:S(2)}, u32[]{:S(2)}) async-start(bf16[4,48,2064]{2,1,0:T(8,128)(2,1)} %pad_maximum_fusion.4), calls=%async_computation.4 | async-start | bytes 1671168 | tf_op jit(solution)/shard_map/all_to_all | solution.py:828
  313.7 6.0 %collective-permute-start.27 = (f32[1,128,1536]{2,1,0:T(8,128)S(1)}, f32[1,128,1536]{2,1,0:T(8,128)S(1)}, u32[]{:S(2)}, u32[]{:S(2)}) collective-permute-start(f32[1,128,1536]{2,1,0:T(8,128)S(1)} %get-tuple-element.270), channel_id=1, source_target_pairs={{0,1},{1,0},{2,3},{3,2},{4,5},{5,4},{6,7},{7,6},{8,9},{9,8},{10,11... | collective-permute-start | bytes 2359304 | tf_op jit(solution)/shard_map/ppermute | solution.py:809
  313.9 6.2 %collective-permute-start.26 = (f32[1,128,1536]{2,1,0:T(8,128)S(1)}, f32[1,128,1536]{2,1,0:T(8,128)S(1)}, u32[]{:S(2)}, u32[]{:S(2)}) collective-permute-start(f32[1,128,1536]{2,1,0:T(8,128)S(1)} %get-tuple-element.273), channel_id=1, source_target_pairs={{0,1},{1,0},{2,3},{3,2},{4,5},{5,4},{6,7},{7,6},{8,9},{9,8},{10,11... | collective-permute-start | bytes 2359304 | tf_op jit(solution)/shard_map/ppermute | solution.py:809
  315.4 4.3 %copy-start.17 = (bf16[2,128,1536]{2,1,0:T(8,128)(2,1)S(1)}, bf16[2,128,1536]{2,1,0:T(8,128)(2,1)}, u32[]{:S(2)}) copy-start(bf16[2,128,1536]{2,1,0:T(8,128)(2,1)} %param.20) | copy-start | bytes 2359300
  322.7 9.6 %copy-start.4 = (f32[48,6448]{1,0:T(8,128)S(1)}, f32[48,6448]{1,0:T(8,128)}, u32[]{:S(2)}) copy-start(f32[48,6448]{1,0:T(8,128)} %first_ref.1) | copy-start | bytes 3714052
  333.6 3.7 %copy-start.45 = (bf16[384]{0:T(512)(128)(2,1)S(1)}, bf16[384]{0:T(512)(128)(2,1)}, u32[]{:S(2)}) copy-start(bf16[384]{0:T(512)(128)(2,1)} %param.22) | copy-start | bytes 2308
  333.6 3.7 %copy-start.52 = (f32[48]{0:T(128)S(1)}, f32[48]{0:T(128)}, u32[]{:S(2)}) copy-start(f32[48]{0:T(128)} %param.24) | copy-start | bytes 580
  333.6 3.7 %copy-start.53 = (f32[48]{0:T(128)S(1)}, f32[48]{0:T(128)}, u32[]{:S(2)}) copy-start(f32[48]{0:T(128)} %param.23) | copy-start | bytes 580
  333.6 4.3 %copy-start.46 = (f32[3,12]{1,0:T(4,128)S(1)}, f32[3,12]{1,0:T(4,128)}, u32[]{:S(2)}) copy-start(f32[3,12]{1,0:T(4,128)} %param.33) | copy-start | bytes 436
  333.6 4.3 %copy-start.47 = (f32[3,12]{1,0:T(4,128)S(1)}, f32[3,12]{1,0:T(4,128)}, u32[]{:S(2)}) copy-start(f32[3,12]{1,0:T(4,128)} %param.32) | copy-start | bytes 436
  333.6 4.3 %copy-start.49 = (bf16[3,12]{1,0:T(4,128)(2,1)S(1)}, bf16[3,12]{1,0:T(4,128)(2,1)}, u32[]{:S(2)}) copy-start(bf16[3,12]{1,0:T(4,128)(2,1)} %param.31) | copy-start | bytes 220
  333.6 5.0 %copy-start.41 = (f32[5,104]{1,0:T(8,128)S(1)}, f32[5,104]{1,0:T(8,128)}, u32[]{:S(2)}) copy-start(f32[5,104]{1,0:T(8,128)} %param.30) | copy-start | bytes 6244
  333.6 5.0 %copy-start.42 = (f32[5,104]{1,0:T(8,128)S(1)}, f32[5,104]{1,0:T(8,128)}, u32[]{:S(2)}) copy-start(f32[5,104]{1,0:T(8,128)} %param.29) | copy-start | bytes 6244
  (24 other events, 40.8 us)
